TPU v7x, 32 devices: a whole 2x2x4 slice. The times are simulated.
32 devices in a mesh: seq: 16 (over z, x, core), batch: 2 (over y).
Axes of the slice: x: 2, y: 2, z: 4, core: 2. Of those that a mesh axis runs over, the one named last changes fastest.
Arguments:
- inputs: bfloat16 [2, 4096, 1024], P('batch', 'seq'), may hold values from -6 to 6
- grad_out: bfloat16 [2, 4096, 1024], P('batch', 'seq'), may hold values from -6 to 6
- spectrum: float32 [2, 32, 256, 1024], P(None, 'seq', None, 'batch'), may hold values from -6 to 6
- first_moment: float32 [2, 32, 256, 1024], P(None, 'seq', None, 'batch'), may hold values from -2 to 2
- second_moment: float32 [2, 32, 256, 1024], P(None, 'seq', None, 'batch'), may hold values from 0.1 to 4
Outputs:
- new_spectrum: float32 [2, 32, 256, 1024], P(None, 'seq', None, 'batch')
- new_first: float32 [2, 32, 256, 1024], P(None, 'seq', None, 'batch')
- new_second: float32 [2, 32, 256, 1024], P(None, 'seq', None, 'batch')
- filtered: bfloat16 [2, 4096, 1024], P('batch', 'seq')
All inputs are finite; a program needn't handle non-finite values.
Results may differ from a plain program's by a relative error of at most 0.0055.
Values may be sent and summed in bfloat16 or wider, within the bound.
No kernel may reach another device: no remote copies, remote signals or barrier semaphores. Data moves between devices by JAX's collectives and lax.ppermute only.
A program may use at most 64 MiB of HBM per device.

v0:
```python
import math

import jax
import jax.numpy as jnp
from jax import lax
from jax.sharding import PartitionSpec as P

full_turn = 2.0 * math.pi
step_rate = 0.5
epsilon = 1e-06


def angles(numer, modulus):
    return full_turn * (numer % modulus).astype(jnp.float32) / modulus


def phase_pair(first_count, second_count, modulus):
    first_index = jnp.arange(first_count, dtype=jnp.int32)
    second_index = jnp.arange(second_count, dtype=jnp.int32)
    phases = angles(first_index[:, None] * second_index[None, :], modulus)
    return (jnp.cos(phases), jnp.sin(phases))


def local_forward(sequence, seq_count, point_count):
    batch_rows = sequence.shape[0]
    outer_count = 2 * seq_count
    full_length = outer_count * point_count
    values = sequence.reshape(batch_rows, seq_count, point_count, -1).astype(jnp.float32)
    outer_cos, outer_sin = phase_pair(outer_count, seq_count, outer_count)
    real_one = jnp.einsum("ja,bach->bjch", outer_cos, values, precision=lax.Precision.HIGHEST)
    imag_one = -jnp.einsum("ja,bach->bjch", outer_sin, values, precision=lax.Precision.HIGHEST)
    twist_cos, twist_sin = phase_pair(outer_count, point_count, full_length)
    twist_cos = twist_cos[None, :, :, None]
    twist_sin = twist_sin[None, :, :, None]
    real_two = real_one * twist_cos + imag_one * twist_sin
    imag_two = imag_one * twist_cos - real_one * twist_sin
    inner_cos, inner_sin = phase_pair(point_count, point_count, point_count)
    real_out = jnp.einsum(
        "cm,bjch->bjmh", inner_cos, real_two, precision=lax.Precision.HIGHEST
    ) + jnp.einsum("cm,bjch->bjmh", inner_sin, imag_two, precision=lax.Precision.HIGHEST)
    imag_out = jnp.einsum(
        "cm,bjch->bjmh", inner_cos, imag_two, precision=lax.Precision.HIGHEST
    ) - jnp.einsum("cm,bjch->bjmh", inner_sin, real_two, precision=lax.Precision.HIGHEST)
    return (real_out, imag_out)


def local_inverse(real_in, imag_in, seq_count, point_count):
    outer_count = 2 * seq_count
    full_length = outer_count * point_count
    inner_cos, inner_sin = phase_pair(point_count, point_count, point_count)
    real_one = jnp.einsum(
        "mc,bjmh->bjch", inner_cos, real_in, precision=lax.Precision.HIGHEST
    ) - jnp.einsum("mc,bjmh->bjch", inner_sin, imag_in, precision=lax.Precision.HIGHEST)
    imag_one = jnp.einsum(
        "mc,bjmh->bjch", inner_sin, real_in, precision=lax.Precision.HIGHEST
    ) + jnp.einsum("mc,bjmh->bjch", inner_cos, imag_in, precision=lax.Precision.HIGHEST)
    twist_cos, twist_sin = phase_pair(outer_count, point_count, full_length)
    twist_cos = twist_cos[None, :, :, None]
    twist_sin = twist_sin[None, :, :, None]
    real_two = real_one * twist_cos - imag_one * twist_sin
    imag_two = real_one * twist_sin + imag_one * twist_cos
    outer_cos, outer_sin = phase_pair(outer_count, seq_count, outer_count)
    result = jnp.einsum(
        "ja,bjch->bach", outer_cos, real_two, precision=lax.Precision.HIGHEST
    ) - jnp.einsum("ja,bjch->bach", outer_sin, imag_two, precision=lax.Precision.HIGHEST)
    return result / full_length


def channel_layout(inputs, grad_out, spectrum, first_moment, second_moment):
    seq_count = lax.axis_size("seq")
    batch_count = lax.axis_size("batch")
    batch_rows, point_count, channels = inputs.shape
    narrow = channels // (seq_count * batch_count)
    group_width = batch_count * narrow
    outer_count = 2 * seq_count
    full_length = outer_count * point_count
    local_outer = spectrum.shape[1]
    signal_parts = inputs.reshape(batch_rows, point_count, batch_count, seq_count, narrow)
    cotangent_parts = grad_out.reshape(batch_rows, point_count, batch_count, seq_count, narrow)
    signal_cols, cotangent_cols = (
        lax.all_to_all(signal_parts, "seq", split_axis=3, concat_axis=1, tiled=True),
        lax.all_to_all(cotangent_parts, "seq", split_axis=3, concat_axis=1, tiled=True),
    )
    state_shape = (2, local_outer, point_count, seq_count, narrow)
    spec_cols, first_cols, second_cols = (
        lax.all_to_all(
            spectrum.reshape(state_shape), "seq", split_axis=3, concat_axis=1, tiled=True
        ),
        lax.all_to_all(
            first_moment.reshape(state_shape), "seq", split_axis=3, concat_axis=1, tiled=True
        ),
        lax.all_to_all(
            second_moment.reshape(state_shape), "seq", split_axis=3, concat_axis=1, tiled=True
        ),
    )
    own_shape = (2, outer_count, point_count, narrow)
    spec_cols = spec_cols.reshape(own_shape)
    first_cols = first_cols.reshape(own_shape)
    second_cols = second_cols.reshape(own_shape)
    signal_real, signal_imag = local_forward(
        signal_cols.reshape(batch_rows, seq_count * point_count, group_width),
        seq_count,
        point_count,
    )
    cotangent_real, cotangent_imag = local_forward(
        cotangent_cols.reshape(batch_rows, seq_count * point_count, group_width),
        seq_count,
        point_count,
    )
    real_term = jnp.sum(signal_real * cotangent_real + signal_imag * cotangent_imag, axis=0)
    imag_term = jnp.sum(signal_real * cotangent_imag - signal_imag * cotangent_real, axis=0)
    local_grad = (jnp.stack([real_term, imag_term]) / full_length).reshape(
        2, outer_count, point_count, batch_count, narrow
    )
    own_grad = (
        lax.psum_scatter(local_grad.astype(jnp.bfloat16), "batch", scatter_dimension=3, tiled=True)
        .astype(jnp.float32)
        .reshape(own_shape)
    )
    new_first = 0.9 * first_cols + 0.1 * own_grad
    new_second = 0.99 * second_cols + 0.01 * own_grad * own_grad
    new_spectrum = spec_cols - step_rate * jnp.tanh(new_first / (jnp.sqrt(new_second) + epsilon))
    group_filter = lax.all_gather(new_spectrum, "batch", axis=3, tiled=True)
    filter_real = group_filter[0][None]
    filter_imag = group_filter[1][None]
    mixed_real = signal_real * filter_real - signal_imag * filter_imag
    mixed_imag = signal_real * filter_imag + signal_imag * filter_real
    rows_back = local_inverse(mixed_real, mixed_imag, seq_count, point_count)
    rows_back = rows_back.astype(jnp.bfloat16).reshape(
        batch_rows, seq_count * point_count, batch_count, 1, narrow
    )
    back_shape = (2, outer_count, point_count, 1, narrow)
    spec_back, first_back, second_back = (
        lax.all_to_all(
            new_spectrum.reshape(back_shape), "seq", split_axis=1, concat_axis=3, tiled=True
        ),
        lax.all_to_all(
            new_first.reshape(back_shape), "seq", split_axis=1, concat_axis=3, tiled=True
        ),
        lax.all_to_all(
            new_second.reshape(back_shape), "seq", split_axis=1, concat_axis=3, tiled=True
        ),
    )
    filtered = lax.all_to_all(rows_back, "seq", split_axis=1, concat_axis=3, tiled=True)
    final_shape = spectrum.shape
    return (
        spec_back.reshape(final_shape),
        first_back.reshape(final_shape),
        second_back.reshape(final_shape),
        filtered.reshape(batch_rows, point_count, channels),
    )


def per_device(inputs, grad_out, spectrum, first_moment, second_moment):
    return channel_layout(inputs, grad_out, spectrum, first_moment, second_moment)


def solution(mesh):
    return jax.shard_map(
        per_device,
        mesh=mesh,
        in_specs=(
            P("batch", "seq", None),
            P("batch", "seq", None),
            P(None, "seq", None, "batch"),
            P(None, "seq", None, "batch"),
            P(None, "seq", None, "batch"),
        ),
        out_specs=(
            P(None, "seq", None, "batch"),
            P(None, "seq", None, "batch"),
            P(None, "seq", None, "batch"),
            P("batch", "seq", None),
        ),
        check_vma=False,
    )
```

profile of v0, /device:TPU:0, one launch (start us, length us, event | category | flops | bytes accessed | tf_op | source)
XLA Modules:
  0.0 404.5 jit_solution(18138972879335876599)
XLA Ops:
  9.3 7.4 %all-to-all-start.3 = ((bf16[1,256,2,16,32]{1,4,2,0,3:T(8,128)(2,1)}), bf16[1,256,2,16,32]{1,4,2,0,3:T(8,128)(2,1)S(1)}, u32[]{:S(2)}, u32[]{:S(2)}) async-start(bf16[1,256,2,16,32]{1,4,2,0,3:T(8,128)(2,1)} %copy.145), calls=%async_computation.3 | async-start | bytes 1048576 | tf_op jit(solution)/shard_map/all_to_all | solution.py:82
  17.8 13.2 %all-to-all-done.3 = bf16[1,256,2,16,32]{1,4,2,0,3:T(8,128)(2,1)S(1)} async-done(((bf16[1,256,2,16,32]{1,4,2,0,3:T(8,128)(2,1)}), bf16[1,256,2,16,32]{1,4,2,0,3:T(8,128)(2,1)S(1)}, u32[]{:S(2)}, u32[]{:S(2)}) %all-to-all-start.3) | async-done | bytes 524320 | tf_op jit(solution)/shard_map/all_to_all | solution.py:82
  31.0 4.2 %all-to-all-start.2 = ((bf16[1,256,2,16,32]{1,4,2,0,3:T(8,128)(2,1)}), bf16[1,256,2,16,32]{1,4,2,0,3:T(8,128)(2,1)S(1)}, u32[]{:S(2)}, u32[]{:S(2)}) async-start(bf16[1,256,2,16,32]{1,4,2,0,3:T(8,128)(2,1)} %copy.140), calls=%async_computation.2 | async-start | bytes 1048576 | tf_op jit(solution)/shard_map/all_to_all | solution.py:81
  38.6 10.8 %all-to-all-done.2 = bf16[1,256,2,16,32]{1,4,2,0,3:T(8,128)(2,1)S(1)} async-done(((bf16[1,256,2,16,32]{1,4,2,0,3:T(8,128)(2,1)}), bf16[1,256,2,16,32]{1,4,2,0,3:T(8,128)(2,1)S(1)}, u32[]{:S(2)}, u32[]{:S(2)}) %all-to-all-start.2) | async-done | bytes 524320 | tf_op jit(solution)/shard_map/all_to_all | solution.py:81
  49.4 4.2 %all-to-all-start.1 = ((f32[2,2,256,16,32]{2,4,1,0,3:T(8,128)}), f32[2,2,256,16,32]{2,4,1,0,3:T(8,128)S(1)}, u32[]{:S(2)}, u32[]{:S(2)}) async-start(f32[2,2,256,16,32]{2,4,1,0,3:T(8,128)} %copy.137), calls=%async_computation.1 | async-start | bytes 4194304 | tf_op jit(solution)/shard_map/all_to_all | solution.py:89
  67.6 26.9 %all-to-all-done.1 = f32[2,2,256,16,32]{2,4,1,0,3:T(8,128)S(1)} async-done(((f32[2,2,256,16,32]{2,4,1,0,3:T(8,128)}), f32[2,2,256,16,32]{2,4,1,0,3:T(8,128)S(1)}, u32[]{:S(2)}, u32[]{:S(2)}) %all-to-all-start.1) | async-done | bytes 2097184 | tf_op jit(solution)/shard_map/all_to_all | solution.py:89
  95.9 11.3 %all-to-all-start.4 = ((f32[2,2,256,16,32]{2,4,1,0,3:T(8,128)}), f32[2,2,256,16,32]{2,4,1,0,3:T(8,128)}, u32[]{:S(2)}, u32[]{:S(2)}) async-start(f32[2,2,256,16,32]{2,4,1,0,3:T(8,128)} %copy.156), calls=%async_computation.5 | async-start | bytes 4194304 | tf_op jit(solution)/shard_map/all_to_all | solution.py:92
  107.4 4.7 %fusion.35 = (f32[32,256,64]{1,0,2:T(8,128)S(1)}, f32[32,256,64]{1,0,2:T(8,128)S(1)}, f32[32,256,64]{1,0,2:T(8,128)S(1)}, f32[32,256,64]{1,0,2:T(8,128)S(1)}) fusion(f32[32,256,64]{1,0,2:T(8,128)} %fusion.134, f32[32,256]{1,0:T(8,128)S(1)} %get-tuple-element.35, f32[32,256]{1,0:T(8,128)S(1)} %get-tuple-element.36, f32[32,256,64]{1,0,2:T(8,128)} %fusion.137, ...), kind=kOutput, calls=%fused_computation.59 | convolution fusion | flops 108010496 | bytes 15269888 | tf_op jit(solution)/shard_map/ja,bach->bjch/dot_general | solution.py:30
  112.1 3.8 fusion.52
  116.0 3.8 fusion.50
  119.7 4.2 %fusion.42 = f32[32,64,256]{2,1,0:T(8,128)S(1)} fusion(f32[32,256,64]{1,0,2:T(8,128)S(1)} %get-tuple-element.33), kind=kOutput, calls=%fused_computation.71 | convolution fusion | flops 1611530240 | bytes 4194304 | tf_op jit(solution)/shard_map/cm,bjch->bjmh/dot_general | solution.py:41
  123.9 3.8 fusion.44
  127.7 3.9 fusion.58
  131.6 4.0 fusion.61
  135.6 3.8 fusion.67
  139.4 4.1 %fusion.26 = (f32[1,32,256,64]{2,3,1,0:T(8,128)S(1)}, f32[1,32,256,64]{2,3,1,0:T(8,128)S(1)}) fusion(f32[32,64,256]{2,1,0:T(8,128)S(1)} %fusion.61, f32[32,64,256]{2,1,0:T(8,128)S(1)} %fusion.67, f32[32,64,256]{2,1,0:T(8,128)S(1)} %fusion.58, f32[32,64,256]{2,1,0:T(8,128)S(1)} %fusion.44, f32[32,256,64]{1,0,2:T(8,128)S(1)} %get-tuple-element.34), kind=kOutput, calls=%fused_computation.38 | convolution fusion | flops 1615200256 | bytes 14680064 | tf_op jit(solution)/shard_map/cm,bjch->bjmh/dot_general | solution.py:38
  151.6 7.9 %all-to-all-start = ((f32[2,2,256,16,32]{2,4,1,0,3:T(8,128)}), f32[2,2,256,16,32]{2,4,1,0,3:T(8,128)}, u32[]{:S(2)}, u32[]{:S(2)}) async-start(f32[2,2,256,16,32]{2,4,1,0,3:T(8,128)} %copy.134), calls=%async_computation | async-start | bytes 4194304 | tf_op jit(solution)/shard_map/all_to_all | solution.py:86
  166.1 34.5 %all-to-all-done = f32[2,2,256,16,32]{2,4,1,0,3:T(8,128)} async-done(((f32[2,2,256,16,32]{2,4,1,0,3:T(8,128)}), f32[2,2,256,16,32]{2,4,1,0,3:T(8,128)}, u32[]{:S(2)}, u32[]{:S(2)}) %all-to-all-start) | async-done | bytes 2097184 | tf_op jit(solution)/shard_map/all_to_all | solution.py:86
  203.7 6.5 %multiply_subtract_fusion = (f32[2,32,256,1,32]{2,4,1,0,3:T(8,128)S(1)}, f32[2,32,256,1,32]{2,4,1,0,3:T(8,128)}, f32[2,32,256,1,32]{2,4,1,0,3:T(8,128)}) fusion(f32[2,32,256,1,32]{2,4,1,0,3:T(8,128)} %bitcast.283, f32[2,32,256,1,32]{2,4,1,0,3:T(8,128)} %bitcast.281, bf16[2,32,256,1,32]{2,4,1,0,3:T(8,128)(2,1)} %reduce-scatter.2.cloned.1.call-done, ...), kind=kLoop, calls=%fused_computation.68 | loop fusion | flops 5242880 | bytes 13631488 | tf_op jit(solution)/shard_map/sub | solution.py:122
  211.7 11.3 %all-to-all-start.5 = ((f32[2,32,256,1,32]{2,4,0,3,1:T(8,128)}), f32[2,32,256,1,32]{2,4,0,3,1:T(8,128)}, u32[]{:S(2)}, u32[]{:S(2)}) async-start(f32[2,32,256,1,32]{2,4,0,3,1:T(8,128)} %copy.158), calls=%async_computation.6 | async-start | bytes 4194304 | tf_op jit(solution)/shard_map/all_to_all | solution.py:134
  223.0 3.2 copy.161
  226.2 37.8 %all-to-all-done.5 = f32[2,32,256,1,32]{2,4,0,3,1:T(8,128)} async-done(((f32[2,32,256,1,32]{2,4,0,3,1:T(8,128)}), f32[2,32,256,1,32]{2,4,0,3,1:T(8,128)}, u32[]{:S(2)}, u32[]{:S(2)}) %all-to-all-start.5) | async-done | bytes 2097184 | tf_op jit(solution)/shard_map/all_to_all | solution.py:134
  264.0 11.3 %all-to-all-start.6 = ((f32[2,32,256,1,32]{2,4,0,3,1:T(8,128)}), f32[2,32,256,1,32]{2,4,0,3,1:T(8,128)}, u32[]{:S(2)}, u32[]{:S(2)}) async-start(f32[2,32,256,1,32]{2,4,0,3,1:T(8,128)} %copy.161), calls=%async_computation.7 | async-start | bytes 4194304 | tf_op jit(solution)/shard_map/all_to_all | solution.py:137
  275.4 5.5 %fusion.8 = f32[2,32,256,32]{2,3,1,0:T(8,128)} fusion(f32[2,32,256,32]{2,3,1,0:T(8,128)} %bitcast.284, f32[2,32,256,32]{2,3,1,0:T(8,128)} %bitcast.280, bf16[2,32,256,1,32]{2,4,1,0,3:T(8,128)(2,1)S(1)} %copy-done.2, f32[2,32,256,32]{2,3,1,0:T(8,128)} %bitcast.282), kind=kLoop, calls=%fused_computation.14 | loop fusion | flops 5242880 | bytes 9437184 | tf_op jit(solution)/shard_map/sub | solution.py:122
  284.0 32.3 %all-to-all-done.6 = f32[2,32,256,1,32]{2,4,0,3,1:T(8,128)} async-done(((f32[2,32,256,1,32]{2,4,0,3,1:T(8,128)}), f32[2,32,256,1,32]{2,4,0,3,1:T(8,128)}, u32[]{:S(2)}, u32[]{:S(2)}) %all-to-all-start.6) | async-done | bytes 2097184 | tf_op jit(solution)/shard_map/all_to_all | solution.py:137
  316.3 11.7 %all-to-all-start.7 = ((f32[2,32,256,1,32]{2,4,0,3,1:T(8,128)}), f32[2,32,256,1,32]{2,4,0,3,1:T(8,128)}, u32[]{:S(2)}, u32[]{:S(2)}) async-start(f32[2,32,256,1,32]{2,4,0,3,1:T(8,128)} %copy.164), calls=%async_computation.8 | async-start | bytes 4194304 | tf_op jit(solution)/shard_map/all_to_all | solution.py:140
  328.0 11.0 %all-gather.2.cloned.1.call-done = f32[2,32,256,64]{2,3,1,0:T(8,128)} async-done(((f32[2,32,256,32]{2,3,1,0:T(8,128)}), f32[2,32,256,64]{2,3,1,0:T(8,128)}) %all-gather.2.cloned.1.call-update) | async-done | bytes 4194320 | tf_op jit(solution)/shard_map/all_gather | solution.py:123
  339.0 3.7 fusion.28
  351.4 3.4 fusion.15
  365.4 3.2 all-to-all-done.7
  368.6 11.2 %all-to-all-start.8 = ((bf16[16,2,8192]{2,1,0:T(2,128)(2,1)}), bf16[16,2,8192]{2,1,0:T(2,128)(2,1)S(1)}, u32[]{:S(2)}, u32[]{:S(2)}) async-start(bf16[16,2,8192]{2,1,0:T(2,128)(2,1)} %reshape.247), calls=%async_computation.9 | async-start | bytes 1048576 | tf_op jit(solution)/shard_map/all_to_all | solution.py:144
  390.9 3.2 all-to-all-done.8
  (58 shorter events, 78.3 us)
Async XLA Ops:
  7.2 9.5 %copy-start.3 = (bf16[1,256,1024]{2,1,0:T(8,128)(2,1)S(1)}, bf16[1,256,1024]{2,1,0:T(8,128)(2,1)}, u32[]{:S(2)}) copy-start(bf16[1,256,1024]{2,1,0:T(8,128)(2,1)} %param.5) | copy-start | bytes 1572868
  9.3 21.7 %all-to-all-start.3 = ((bf16[1,256,2,16,32]{1,4,2,0,3:T(8,128)(2,1)}), bf16[1,256,2,16,32]{1,4,2,0,3:T(8,128)(2,1)S(1)}, u32[]{:S(2)}, u32[]{:S(2)}) async-start(bf16[1,256,2,16,32]{1,4,2,0,3:T(8,128)(2,1)} %copy.145), calls=%async_computation.3 | async-start | bytes 1048576 | tf_op jit(solution)/shard_map/all_to_all | solution.py:82
  31.0 18.4 %all-to-all-start.2 = ((bf16[1,256,2,16,32]{1,4,2,0,3:T(8,128)(2,1)}), bf16[1,256,2,16,32]{1,4,2,0,3:T(8,128)(2,1)S(1)}, u32[]{:S(2)}, u32[]{:S(2)}) async-start(bf16[1,256,2,16,32]{1,4,2,0,3:T(8,128)(2,1)} %copy.140), calls=%async_computation.2 | async-start | bytes 1048576 | tf_op jit(solution)/shard_map/all_to_all | solution.py:81
  49.4 45.1 %all-to-all-start.1 = ((f32[2,2,256,16,32]{2,4,1,0,3:T(8,128)}), f32[2,2,256,16,32]{2,4,1,0,3:T(8,128)S(1)}, u32[]{:S(2)}, u32[]{:S(2)}) async-start(f32[2,2,256,16,32]{2,4,1,0,3:T(8,128)} %copy.137), calls=%async_computation.1 | async-start | bytes 4194304 | tf_op jit(solution)/shard_map/all_to_all | solution.py:89
  94.6 1.3 copy-start.1
  95.9 55.7 %all-to-all-start.4 = ((f32[2,2,256,16,32]{2,4,1,0,3:T(8,128)}), f32[2,2,256,16,32]{2,4,1,0,3:T(8,128)}, u32[]{:S(2)}, u32[]{:S(2)}) async-start(f32[2,2,256,16,32]{2,4,1,0,3:T(8,128)} %copy.156), calls=%async_computation.5 | async-start | bytes 4194304 | tf_op jit(solution)/shard_map/all_to_all | solution.py:92
  107.2 96.5 %reduce-scatter.2.cloned.1.call-start = ((), (), s32[]{:S(2)}) async-start(), calls=%async_computation.10 | async-start | bytes 3145728 | tf_op jit(solution)/shard_map/reduce_scatter | solution.py:116
  135.6 3.8 copy-start
  151.6 48.9 %all-to-all-start = ((f32[2,2,256,16,32]{2,4,1,0,3:T(8,128)}), f32[2,2,256,16,32]{2,4,1,0,3:T(8,128)}, u32[]{:S(2)}, u32[]{:S(2)}) async-start(f32[2,2,256,16,32]{2,4,1,0,3:T(8,128)} %copy.134), calls=%async_computation | async-start | bytes 4194304 | tf_op jit(solution)/shard_map/all_to_all | solution.py:86
  211.7 52.3 %all-to-all-start.5 = ((f32[2,32,256,1,32]{2,4,0,3,1:T(8,128)}), f32[2,32,256,1,32]{2,4,0,3,1:T(8,128)}, u32[]{:S(2)}, u32[]{:S(2)}) async-start(f32[2,32,256,1,32]{2,4,0,3,1:T(8,128)} %copy.158), calls=%async_computation.6 | async-start | bytes 4194304 | tf_op jit(solution)/shard_map/all_to_all | solution.py:134
  226.2 49.2 %copy-start.2 = (bf16[2,32,256,1,32]{2,4,1,0,3:T(8,128)(2,1)S(1)}, bf16[2,32,256,1,32]{2,4,1,0,3:T(8,128)(2,1)}, u32[]{:S(2)}) copy-start(bf16[2,32,256,1,32]{2,4,1,0,3:T(8,128)(2,1)} %reduce-scatter.2.cloned.1.call-done) | copy-start | bytes 3145732
  264.0 52.3 %all-to-all-start.6 = ((f32[2,32,256,1,32]{2,4,0,3,1:T(8,128)}), f32[2,32,256,1,32]{2,4,0,3,1:T(8,128)}, u32[]{:S(2)}, u32[]{:S(2)}) async-start(f32[2,32,256,1,32]{2,4,0,3,1:T(8,128)} %copy.161), calls=%async_computation.7 | async-start | bytes 4194304 | tf_op jit(solution)/shard_map/all_to_all | solution.py:137
  275.3 63.7 %all-gather.2.cloned.1.call-start = ((), (), s32[]{:S(2)}) async-start(), calls=%async_computation.11 | async-start | bytes 6291456 | tf_op jit(solution)/shard_map/all_gather | solution.py:123
  316.3 52.3 %all-to-all-start.7 = ((f32[2,32,256,1,32]{2,4,0,3,1:T(8,128)}), f32[2,32,256,1,32]{2,4,0,3,1:T(8,128)}, u32[]{:S(2)}, u32[]{:S(2)}) async-start(f32[2,32,256,1,32]{2,4,0,3,1:T(8,128)} %copy.164), calls=%async_computation.8 | async-start | bytes 4194304 | tf_op jit(solution)/shard_map/all_to_all | solution.py:140
  368.6 25.5 %all-to-all-start.8 = ((bf16[16,2,8192]{2,1,0:T(2,128)(2,1)}), bf16[16,2,8192]{2,1,0:T(2,128)(2,1)S(1)}, u32[]{:S(2)}, u32[]{:S(2)}) async-start(bf16[16,2,8192]{2,1,0:T(2,128)(2,1)} %reshape.247), calls=%async_computation.9 | async-start | bytes 1048576 | tf_op jit(solution)/shard_map/all_to_all | solution.py:144
Sparse Core Ops, SparseCore 0:
  145.7 33.1 reduce-scatter.1
  281.0 58.0 all-gather.1
where the time goes:
time: 410 us; the launch traced here: 405 us
  waiting for transfers between devices  173 us (42%)
  starting transfers between devices  80.6 us (20%)
  matrix products  60.1 us (15%)
  local copies, waits for them, and re-layouts  54.6 us (13%)
  other arithmetic  21.5 us (5%)
  between operations  14.6 us (4%)
    all_to_all x1, waiting for transfers between devices, channel_layout(): lax.all_to_all(new_spectrum.reshape(back_shape), 'seq', split_axis=1, con...  37.8 us
    all_to_all x1, waiting for transfers between devices, channel_layout(): lax.all_to_all(spectrum.reshape(state_shape), 'seq', split_axis=3, concat...  34.5 us
    all_to_all x1, waiting for transfers between devices, channel_layout(): lax.all_to_all(new_first.reshape(back_shape), 'seq', split_axis=1, concat...  32.3 us
    all_to_all x1, waiting for transfers between devices, channel_layout(): lax.all_to_all(first_moment.reshape(state_shape), 'seq', split_axis=3, co...  26.9 us
    unnamed x19, local copies, waits for them, and re-layouts  20.7 us
    all_to_all x1, waiting for transfers between devices, channel_layout(): lax.all_to_all(cotangent_parts, 'seq', split_axis=3, concat_axis=1, tiled...  13.2 us
    sub x2, other arithmetic, channel_layout(): spec_cols - step_rate * jnp.tanh(new_first / (jnp.sqrt(new_second) + epsi...  12 us
    all_to_all x1, starting transfers between devices, channel_layout(): lax.all_to_all(new_second.reshape(back_shape), 'seq', split_axis=1, conca...  11.7 us
  transfers between devices with their start and end apart: 11, of which 9 were waited for; matrix products, arithmetic and copies ran while one was open for 30% of the time, Pallas kernels for 0%

commit v1 on v0

v1 whole, which is shorter than its diff:
```python
import functools
import math

import jax
import jax.numpy as jnp
import numpy as np
from jax import lax
from jax.experimental import pallas as pl
from jax.experimental.pallas import tpu as pltpu
from jax.sharding import PartitionSpec as P

step_rate = 0.5
epsilon = 1e-06
sub = 16
lane = 128


def turn_table(numer, modulus):
    phase = 2.0 * math.pi * (numer % modulus) / modulus
    return np.cos(phase), np.sin(phase)


def twist_table(outer, points):
    half = outer // 2
    index = np.arange(half + 1)[:, None] * np.arange(points)[None, :]
    cos, sin = turn_table(index, outer * points)
    return np.stack([cos, sin], axis=1).astype(np.float32)


def point_matrices(points, scale_back):
    index = np.arange(points)[:, None] * np.arange(points)[None, :]
    cos, sin = turn_table(index, points)
    ahead = np.block([[cos, -sin], [sin, cos]])
    back = np.block([[cos, sin], [-sin, cos]]) * scale_back
    return ahead.astype(np.float32), back.astype(np.float32)


def times_phase(re, im, turns, count):
    if turns == 0:
        return re, im
    if 4 * turns == count:
        return im, -re
    cos = math.cos(2.0 * math.pi * turns / count)
    sin = math.sin(2.0 * math.pi * turns / count)
    return re * cos + im * sin, im * cos - re * sin


def half_spectrum(values):
    total = 2 * len(values)
    if total == 2:
        return [(values[0], None), (values[0], None)]
    even = half_spectrum(values[0::2])
    odd = half_spectrum(values[1::2])
    quarter = total // 4
    out = [None] * (total // 2 + 1)
    for index in range(quarter + 1):
        even_re, even_im = even[index]
        odd_re, odd_im = odd[index]
        if index == 0:
            out[0] = (even_re + odd_re, None)
            out[total // 2] = (even_re - odd_re, None)
        elif index == quarter:
            out[index] = (even_re, -odd_re)
        else:
            turned_re, turned_im = times_phase(odd_re, odd_im, index, total)
            out[index] = (even_re + turned_re, even_im + turned_im)
            out[total // 2 - index] = (even_re - turned_re, turned_im - even_im)
    return out


def real_segments(bins):
    count = 2 * (len(bins) - 1)
    if count == 2:
        return [bins[0][0] + bins[1][0]]
    quarter = count // 4
    even = [None] * (quarter + 1)
    odd = [None] * (quarter + 1)
    for index in range(quarter + 1):
        low_re, low_im = bins[index]
        high_re, high_im = bins[count // 2 - index]
        if index == 0:
            even[0] = (low_re + high_re, None)
            odd[0] = (low_re - high_re, None)
        elif index == quarter:
            even[index] = (low_re, None)
            odd[index] = (-low_im, None)
        else:
            even[index] = (low_re + high_re, low_im - high_im)
            diff_re, diff_im = low_re - high_re, low_im + high_im
            cos = math.cos(2.0 * math.pi * index / count)
            sin = math.sin(2.0 * math.pi * index / count)
            odd[index] = (diff_re * cos - diff_im * sin, diff_re * sin + diff_im * cos)
    first = real_segments(even)
    second = real_segments(odd)
    return [item for pair in zip(first, second) for item in pair]


both_last = (((1,), (1,)), ((), ()))
both_first = (((0,), (0,)), ((), ()))


def square_eye(points, flipped):
    row = lax.broadcasted_iota(jnp.int32, (points, points), 0)
    col = lax.broadcasted_iota(jnp.int32, (points, points), 1)
    picked = jnp.where(flipped, points - 1 - col, col)
    return jnp.where(row == picked, 1.0, 0.0).astype(jnp.bfloat16)


def pack_kernel(signal_ref, cotangent_ref, out_ref, *, narrow):
    points, width = signal_ref.shape
    eye = square_eye(width, False)
    for part, source in enumerate((signal_ref, cotangent_ref)):
        turned = lax.dot_general(eye, source[...], both_last, preferred_element_type=jnp.float32)
        turned = turned.astype(jnp.bfloat16).reshape(width // narrow, narrow, points)
        out_ref[:, part * narrow : (part + 1) * narrow, :] = turned


def pack_call(signal, cotangent, narrow):
    points, channels = signal.shape
    width = math.gcd(channels, 256)
    return pl.pallas_call(
        functools.partial(pack_kernel, narrow=narrow),
        grid=(channels // width,),
        in_specs=[pl.BlockSpec((points, width), lambda step: (0, step))] * 2,
        out_specs=pl.BlockSpec((width // narrow, 2 * narrow, points), lambda step: (step, 0, 0)),
        out_shape=jax.ShapeDtypeStruct((channels // narrow, 2 * narrow, points), jnp.bfloat16),
        name="pack",
    )(signal, cotangent)


def unpack_kernel(in_ref, out_ref):
    eye = square_eye(out_ref.shape[0], False)
    out_ref[...] = lax.dot_general(
        eye, in_ref[...], both_last, preferred_element_type=jnp.float32
    ).astype(jnp.bfloat16)


def unpack_call(rows):
    channels, points = rows.shape
    width = math.gcd(channels, 256)
    return pl.pallas_call(
        unpack_kernel,
        grid=(channels // width,),
        in_specs=[pl.BlockSpec((width, points), lambda step: (step, 0))],
        out_specs=pl.BlockSpec((points, width), lambda step: (0, step)),
        out_shape=jax.ShapeDtypeStruct((points, channels), jnp.bfloat16),
        name="unpack",
    )(rows)


def forward_kernel(in_ref, twist_ref, matrix_ref, grad_ref, spectra_ref, mid_ref, *, scale):
    sequences, segments, pair_rows, points = in_ref.shape
    narrow = pair_rows // 2
    rows = sequences * narrow
    tiles = pair_rows // sub
    residue = pl.program_id(0)

    @pl.when(residue == 0)
    def _():
        def tile_step(step, carry):
            which = step // tiles
            piece = step % tiles
            start = pl.multiple_of(piece * sub, sub)
            target = (piece // (tiles // 2)) * rows + which * narrow
            target = pl.multiple_of(target + (piece % (tiles // 2)) * sub, sub)
            for left in range(0, points, lane):
                values = [
                    in_ref[which, seg, pl.ds(start, sub), left : left + lane].astype(jnp.float32)
                    for seg in range(segments)
                ]
                for index, (re, im) in enumerate(half_spectrum(values)):
                    cos = twist_ref[index, 0:1, left : left + lane]
                    sin = twist_ref[index, 1:2, left : left + lane]
                    if im is None:
                        new_re, new_im = re * cos, -(re * sin)
                    else:
                        new_re, new_im = re * cos + im * sin, im * cos - re * sin
                    mid_ref[index, pl.ds(target, sub), left : left + lane] = new_re.astype(jnp.bfloat16)
                    mid_ref[index, pl.ds(target, sub), points + left : points + left + lane] = (
                        new_im.astype(jnp.bfloat16)
                    )
            return carry

        lax.fori_loop(0, sequences * tiles, tile_step, 0)

    full = jnp.dot(mid_ref[residue], matrix_ref[0], preferred_element_type=jnp.float32)
    full = full + jnp.dot(mid_ref[residue], matrix_ref[1], preferred_element_type=jnp.float32)
    signal_re, signal_im = full[:rows, :points], full[:rows, points:]
    cotan_re, cotan_im = full[rows:, :points], full[rows:, points:]
    spectra_ref[0, 0] = signal_re
    spectra_ref[0, 1] = signal_im
    real_term = signal_re * cotan_re + signal_im * cotan_im
    imag_term = signal_re * cotan_im - signal_im * cotan_re
    real_sum = jnp.sum(real_term.reshape(sequences, narrow, points), axis=0) * scale
    imag_sum = jnp.sum(imag_term.reshape(sequences, narrow, points), axis=0) * scale
    grad_ref[residue, 0] = real_sum.astype(jnp.bfloat16)
    grad_ref[residue, 1] = imag_sum.astype(jnp.bfloat16)

    @pl.when(jnp.logical_and(residue > 0, residue < segments))
    def _():
        grad_ref[2 * segments - residue, 0] = real_sum.astype(jnp.bfloat16)
        grad_ref[2 * segments - residue, 1] = (-imag_sum).astype(jnp.bfloat16)


def forward_call(arrived, twist, matrices):
    sequences, segments, pair_rows, points = arrived.shape
    narrow = pair_rows // 2
    outer = 2 * segments
    rows = sequences * narrow
    fixed4 = lambda step: (0, 0, 0, 0)
    fixed3 = lambda step: (0, 0, 0)
    return pl.pallas_call(
        functools.partial(forward_kernel, scale=1.0 / (outer * points)),
        grid=(segments + 1,),
        in_specs=[
            pl.BlockSpec(arrived.shape, fixed4),
            pl.BlockSpec(twist.shape, fixed3),
            pl.BlockSpec(matrices.shape, fixed3),
        ],
        out_specs=[
            pl.BlockSpec((outer, 2, narrow, points), fixed4),
            pl.BlockSpec((1, 2, rows, points), lambda step: (step, 0, 0, 0)),
        ],
        out_shape=[
            jax.ShapeDtypeStruct((outer, 2, narrow, points), jnp.bfloat16),
            jax.ShapeDtypeStruct((segments + 1, 2, rows, points), jnp.float32),
        ],
        scratch_shapes=[pltpu.VMEM((segments + 1, 2 * rows, 2 * points), jnp.bfloat16)],
        name="forward",
    )(arrived, twist, matrices)


def update_kernel(
    flip_ref, grad_ref, spec_ref, first_ref, second_ref, new_spec_ref, new_first_ref, new_second_ref, out_ref
):
    points, width = spec_ref.shape[2:]
    blocks, _, _, narrow, _ = grad_ref.shape
    eye = square_eye(points, flip_ref[pl.program_id(0)] > 0)
    for part in range(2):
        sent = grad_ref[:, 0, part].reshape(width, points)
        grad = lax.dot_general(eye, sent, both_last, preferred_element_type=jnp.float32)
        new_first = 0.9 * first_ref[part, 0] + 0.1 * grad
        new_second = 0.99 * second_ref[part, 0] + 0.01 * grad * grad
        new_spec = spec_ref[part, 0] - step_rate * jnp.tanh(new_first / (jnp.sqrt(new_second) + epsilon))
        new_spec_ref[part, 0] = new_spec
        new_first_ref[part, 0] = new_first
        new_second_ref[part, 0] = new_second
        turned = lax.dot_general(
            new_spec.astype(jnp.bfloat16), eye, both_first, preferred_element_type=jnp.float32
        )
        out_ref[:, 0, part] = turned.astype(jnp.bfloat16).reshape(blocks, narrow, points)


def update_call(flips, sent, spectrum, first_moment, second_moment, width):
    groups, local_outer, _, narrow, points = sent.shape
    channels = spectrum.shape[3]
    blocks = width // narrow
    state = pl.BlockSpec((2, 1, points, width), lambda row, col, flags: (0, row, 0, col))
    wire = pl.BlockSpec((blocks, 1, 2, narrow, points), lambda row, col, flags: (col, row, 0, 0, 0))
    return pl.pallas_call(
        update_kernel,
        grid_spec=pltpu.PrefetchScalarGridSpec(
            num_scalar_prefetch=1,
            grid=(local_outer, channels // width),
            in_specs=[wire, state, state, state],
            out_specs=[state, state, state, wire],
        ),
        out_shape=[jax.ShapeDtypeStruct(spectrum.shape, jnp.float32)] * 3
        + [jax.ShapeDtypeStruct(sent.shape, jnp.bfloat16)],
        name="update",
    )(flips, sent, spectrum, first_moment, second_moment)


def inverse_kernel(spectra_ref, filter_ref, twist_ref, matrix_ref, out_ref, mid_ref):
    sequences, segments, narrow, points = out_ref.shape
    rows = sequences * narrow
    residue = pl.program_id(0)
    mirror = lax.rem(2 * segments - residue, 2 * segments)
    paired = jnp.where(jnp.logical_and(residue > 0, residue < segments), 1.0, 0.0)
    filter_re = filter_ref[residue, 0].astype(jnp.float32) + paired * filter_ref[mirror, 0].astype(jnp.float32)
    filter_im = filter_ref[residue, 1].astype(jnp.float32) - paired * filter_ref[mirror, 1].astype(jnp.float32)
    signal_re = spectra_ref[0, 0].reshape(sequences, narrow, points)
    signal_im = spectra_ref[0, 1].reshape(sequences, narrow, points)
    mixed_re = (signal_re * filter_re - signal_im * filter_im).reshape(rows, points)
    mixed_im = (signal_re * filter_im + signal_im * filter_re).reshape(rows, points)
    mixed = jnp.concatenate([mixed_re.astype(jnp.bfloat16), mixed_im.astype(jnp.bfloat16)], axis=1)
    full = jnp.dot(mixed, matrix_ref[0], preferred_element_type=jnp.float32)
    full = full + jnp.dot(mixed, matrix_ref[1], preferred_element_type=jnp.float32)
    cos = twist_ref[residue, 0:1]
    sin = twist_ref[residue, 1:2]
    mid_ref[residue, 0] = full[:, :points] * cos - full[:, points:] * sin
    mid_ref[residue, 1] = full[:, :points] * sin + full[:, points:] * cos

    @pl.when(residue == segments)
    def _():
        tiles = narrow // sub

        def tile_step(step, carry):
            which = step // tiles
            start = pl.multiple_of((step % tiles) * sub, sub)
            source = pl.multiple_of(step * sub, sub)
            for left in range(0, points, lane):
                bins = [
                    tuple(mid_ref[index, part, pl.ds(source, sub), left : left + lane] for part in range(2))
                    for index in range(segments + 1)
                ]
                for seg, value in enumerate(real_segments(bins)):
                    out_ref[which, seg, pl.ds(start, sub), left : left + lane] = value.astype(jnp.bfloat16)
            return carry

        lax.fori_loop(0, sequences * tiles, tile_step, 0)


def inverse_call(spectra, filters, twist, matrices):
    residues, _, rows, points = spectra.shape
    segments = residues - 1
    narrow = filters.shape[2]
    sequences = rows // narrow
    fixed4 = lambda step: (0, 0, 0, 0)
    fixed3 = lambda step: (0, 0, 0)
    return pl.pallas_call(
        inverse_kernel,
        grid=(residues,),
        in_specs=[
            pl.BlockSpec((1, 2, rows, points), lambda step: (step, 0, 0, 0)),
            pl.BlockSpec(filters.shape, fixed4),
            pl.BlockSpec(twist.shape, fixed3),
            pl.BlockSpec(matrices.shape, fixed3),
        ],
        out_specs=pl.BlockSpec((sequences, segments, narrow, points), fixed4),
        out_shape=jax.ShapeDtypeStruct((sequences, segments, narrow, points), jnp.bfloat16),
        scratch_shapes=[pltpu.VMEM((residues, 2, rows, points), jnp.float32)],
        name="inverse",
    )(spectra, filters, twist, matrices)


def pack_plain(signal, cotangent, narrow):
    points, channels = signal.shape
    both = jnp.stack([signal, cotangent]).reshape(2, points, channels // narrow, narrow)
    return both.transpose(2, 0, 3, 1).reshape(channels // narrow, 2 * narrow, points)


def split_dot(values, matrices):
    first = jnp.dot(values, matrices[0], preferred_element_type=jnp.float32)
    return first + jnp.dot(values, matrices[1], preferred_element_type=jnp.float32)


def forward_plain(arrived, twist, matrices):
    sequences, segments, pair_rows, points = arrived.shape
    narrow = pair_rows // 2
    rows = sequences * narrow
    parts = arrived.reshape(sequences, segments, 2, narrow, points).astype(jnp.float32)
    parts = parts.transpose(1, 2, 0, 3, 4).reshape(segments, 2 * rows, points)
    bins = half_spectrum([parts[seg] for seg in range(segments)])
    re = jnp.stack([item[0] for item in bins])
    im = jnp.stack([jnp.zeros_like(item[0]) if item[1] is None else item[1] for item in bins])
    cos, sin = twist[:, 0][:, None], twist[:, 1][:, None]
    mid = jnp.concatenate([re * cos + im * sin, im * cos - re * sin], axis=2).astype(jnp.bfloat16)
    full = split_dot(mid, matrices)
    signal_re, signal_im = full[:, :rows, :points], full[:, :rows, points:]
    cotan_re, cotan_im = full[:, rows:, :points], full[:, rows:, points:]
    shape = (segments + 1, sequences, narrow, points)
    scale = 1.0 / (2 * segments * points)
    real = jnp.sum((signal_re * cotan_re + signal_im * cotan_im).reshape(shape), axis=1) * scale
    imag = jnp.sum((signal_re * cotan_im - signal_im * cotan_re).reshape(shape), axis=1) * scale
    real = jnp.concatenate([real, real[1:segments][::-1]])
    imag = jnp.concatenate([imag, -imag[1:segments][::-1]])
    grad = jnp.stack([real, imag], axis=1).astype(jnp.bfloat16)
    return grad, jnp.stack([signal_re, signal_im], axis=1)


def update_plain(flips, sent, spectrum, first_moment, second_moment):
    groups, local_outer, _, narrow, points = sent.shape
    flipped = (flips > 0)[None, :, None, None]
    arrived = sent.astype(jnp.float32).transpose(2, 1, 4, 0, 3).reshape(spectrum.shape)
    grad = jnp.where(flipped, arrived[:, :, ::-1], arrived)
    new_first = 0.9 * first_moment + 0.1 * grad
    new_second = 0.99 * second_moment + 0.01 * grad * grad
    new_spec = spectrum - step_rate * jnp.tanh(new_first / (jnp.sqrt(new_second) + epsilon))
    out = jnp.where(flipped, new_spec[:, :, ::-1], new_spec).astype(jnp.bfloat16)
    out = out.reshape(2, local_outer, points, groups, narrow).transpose(3, 1, 0, 4, 2)
    return new_spec, new_first, new_second, out


def inverse_plain(spectra, filters, twist, matrices):
    residues, _, rows, points = spectra.shape
    segments = residues - 1
    narrow = filters.shape[2]
    sequences = rows // narrow
    wide = filters.astype(jnp.float32)
    mirrored = jnp.concatenate([jnp.zeros_like(wide[:1]), wide[segments + 1 :][::-1], jnp.zeros_like(wide[:1])])
    filter_re = (wide[: segments + 1, 0] + mirrored[:, 0])[:, None]
    filter_im = (wide[: segments + 1, 1] - mirrored[:, 1])[:, None]
    shape = (residues, sequences, narrow, points)
    signal_re, signal_im = spectra[:, 0].reshape(shape), spectra[:, 1].reshape(shape)
    mixed_re = (signal_re * filter_re - signal_im * filter_im).reshape(residues, rows, points)
    mixed_im = (signal_re * filter_im + signal_im * filter_re).reshape(residues, rows, points)
    full = split_dot(jnp.concatenate([mixed_re, mixed_im], axis=2).astype(jnp.bfloat16), matrices)
    cos, sin = twist[:, 0][:, None], twist[:, 1][:, None]
    mid_re = full[..., :points] * cos - full[..., points:] * sin
    mid_im = full[..., :points] * sin + full[..., points:] * cos
    out = jnp.stack(real_segments([(mid_re[index], mid_im[index]) for index in range(residues)]))
    out = out.reshape(segments, sequences, narrow, points).transpose(1, 0, 2, 3)
    return out.astype(jnp.bfloat16)


def high_low(matrix):
    high = matrix.astype(jnp.bfloat16)
    low = (matrix - high.astype(np.float32)).astype(jnp.bfloat16)
    return np.stack([high, low])


def per_device(inputs, grad_out, spectrum, first_moment, second_moment):
    seq_count = lax.axis_size("seq")
    batch_count = lax.axis_size("batch")
    batch_rows, points, channels = inputs.shape
    narrow = channels // (seq_count * batch_count)
    local_outer = spectrum.shape[1]
    outer = 2 * seq_count
    tiled = narrow % sub == 0 and points % lane == 0 and batch_rows == 1
    twist = jnp.asarray(twist_table(outer, points))
    ahead, back = point_matrices(points, 1.0 / (outer * points))
    ahead, back = jnp.asarray(high_low(ahead)), jnp.asarray(high_low(back))

    pack = pack_call if tiled else pack_plain
    packed = jnp.stack([pack(inputs[row], grad_out[row], narrow) for row in range(batch_rows)], axis=1)
    arrived = lax.all_to_all(packed, ("batch", "seq"), split_axis=0, concat_axis=0, tiled=True)
    arrived = arrived.reshape(batch_count, seq_count, batch_rows, 2 * narrow, points)
    arrived = arrived.transpose(0, 2, 1, 3, 4).reshape(-1, seq_count, 2 * narrow, points)
    sequences = arrived.shape[0]

    grad, spectra = (forward_call if tiled else forward_plain)(arrived, twist, ahead)
    grad = grad.reshape(seq_count, local_outer, 2, narrow, points)
    sent = lax.all_to_all(grad, "seq", split_axis=0, concat_axis=0, tiled=True)

    residues = lax.axis_index("seq") * local_outer + jnp.arange(local_outer, dtype=jnp.int32)
    flips = (residues > seq_count).astype(jnp.int32)
    update = functools.partial(update_call, width=256) if tiled else update_plain
    new_spectrum, new_first, new_second, filters = update(flips, sent, spectrum, first_moment, second_moment)
    filters = lax.all_to_all(filters, "seq", split_axis=0, concat_axis=0, tiled=True)
    filters = filters.reshape(outer, 2, narrow, points)

    rows = (inverse_call if tiled else inverse_plain)(spectra, filters, twist, back)
    rows = rows.reshape(batch_count, batch_rows, seq_count, narrow, points).transpose(0, 2, 1, 3, 4)
    rows = rows.reshape(batch_count * seq_count, batch_rows, narrow, points)
    rows = lax.all_to_all(rows, ("batch", "seq"), split_axis=0, concat_axis=0, tiled=True)
    if tiled:
        filtered = unpack_call(rows.reshape(channels, points))[None]
    else:
        filtered = rows.transpose(1, 3, 0, 2).reshape(batch_rows, points, channels)
    return new_spectrum, new_first, new_second, filtered


def solution(mesh):
    return jax.shard_map(
        per_device,
        mesh=mesh,
        in_specs=(
            P("batch", "seq", None),
            P("batch", "seq", None),
            P(None, "seq", None, "batch"),
            P(None, "seq", None, "batch"),
            P(None, "seq", None, "batch"),
        ),
        out_specs=(
            P(None, "seq", None, "batch"),
            P(None, "seq", None, "batch"),
            P(None, "seq", None, "batch"),
            P("batch", "seq", None),
        ),
        check_vma=False,
    )
```

time: 410 us -> 157 us (0.38); the launches traced: 405 us -> 156 us
  waiting for transfers between devices: 173 us -> 22.3 us
  blocking collectives: 0 us -> 86.4 us
  starting transfers between devices: 80.6 us -> 3.66 us
  matrix products: 60.1 us -> 0 us
  local copies, waits for them, and re-layouts: 54.6 us -> 1 us
  Pallas kernels: 0 us -> 41.9 us
  other arithmetic: 21.5 us -> 0.52 us
  between operations: 14.6 us -> 0.65 us
    all_to_all x9 -> x1, waiting for transfers between devices: 162 us -> 22.3 us  [per_device(): sent = lax.all_to_all(grad, 'seq', split_axis=0, concat_axis=0, tiled=True)]
    all_to_all x0 -> x3, blocking collectives: none -> 86.4 us  [the longest x1 34.6 us: per_device(): lax.all_to_all(packed, ('batch', 'seq'), split_axis=0, concat_axis=0, til...]
    all_to_all x9 -> x1, starting transfers between devices: 80.3 us -> 3.66 us  [per_device(): sent = lax.all_to_all(grad, 'seq', split_axis=0, concat_axis=0, tiled=True)]
    dot_general x18 -> x0, matrix products: 60.1 us -> none  [the longest x2 7.97 us: local_forward(): jnp.einsum('cm,bjch->bjmh', inner_cos, imag_two, precision=lax.Precision....]
    pallas_call x0 -> x5, Pallas kernels: none -> 41.9 us  [the longest x1 13.1 us: inverse_call(): pl.pallas_call(inverse_kernel, grid=(residues,), in_specs=[pl.BlockSpec((...]
    unnamed x19 -> x2, local copies, waits for them, and re-layouts: 20.7 us -> 1 us
    sub x3 -> x0, other arithmetic: 15.7 us -> none  [the longest x2 12 us: channel_layout(): spec_cols - step_rate * jnp.tanh(new_first / (jnp.sqrt(new_second) + epsi...]
    reshape x7 -> x0, local copies, waits for them, and re-layouts: 12.5 us -> none  [the longest x1 3.16 us: channel_layout(): second_moment.reshape(state_shape)]
  transfers between devices with their start and end apart: 11 -> 1, of which waited for: 9 -> 1; matrix products, arithmetic and copies ran while one was open for 30% -> 0% of each run, Pallas kernels for 0% -> 0%
where the time goes in v1:
time: 157 us; the launch traced here: 156 us
  blocking collectives  86.4 us (55%)
  Pallas kernels  41.9 us (27%)
  waiting for transfers between devices  22.3 us (14%)
  starting transfers between devices  3.66 us (2%)
    all_to_all x1, blocking collectives, per_device(): lax.all_to_all(packed, ('batch', 'seq'), split_axis=0, concat_axis=0, til...  34.6 us
    all_to_all x1, blocking collectives, per_device(): lax.all_to_all(filters, 'seq', split_axis=0, concat_axis=0, tiled=True)  31.5 us
    all_to_all x1, waiting for transfers between devices, per_device(): sent = lax.all_to_all(grad, 'seq', split_axis=0, concat_axis=0, tiled=True)  22.3 us
    all_to_all x1, blocking collectives, per_device(): lax.all_to_all(rows, ('batch', 'seq'), split_axis=0, concat_axis=0, tiled...  20.3 us
    pallas_call x1, Pallas kernels, inverse_call(): pl.pallas_call(inverse_kernel, grid=(residues,), in_specs=[pl.BlockSpec((...  13.1 us
    pallas_call x1, Pallas kernels, forward_call(): pl.pallas_call(functools.partial(forward_kernel, scale=1.0 / (outer * poi...  12.3 us
    pallas_call x1, Pallas kernels, update_call(): pl.pallas_call(update_kernel, grid_spec=pltpu.PrefetchScalarGridSpec(num_...  8.94 us
    pallas_call x1, Pallas kernels, pack_call(): pl.pallas_call(functools.partial(pack_kernel, narrow=narrow), grid=(chann...  3.91 us
  transfers between devices with their start and end apart: 1, of which 1 were waited for; matrix products, arithmetic and copies ran while one was open for 0% of the time, Pallas kernels for 0%

profile of v1, /device:TPU:0, one launch (start us, length us, event | category | flops | bytes accessed | tf_op | source)
XLA Modules:
  0.0 156.5 jit_solution(1487023559922456637)
XLA Ops:
  0.6 3.9 %pack.1 = bf16[32,64,256]{2,1,0:T(8,128)(2,1)} custom-call(bf16[256,1024]{1,0:T(8,128)(2,1)} %bitcast.20, bf16[256,1024]{1,0:T(8,128)(2,1)} %bitcast.21), custom_call_target="tpu_custom_call" | custom-call | tf_op jit(solution)/shard_map/pack/pallas_call | solution.py:121
  4.5 34.6 %all_to_all.20 = bf16[32,1,64,256]{3,2,1,0:T(8,128)(2,1)} all-to-all(bf16[32,1,64,256]{3,2,1,0:T(8,128)(2,1)} %bitcast.14), channel_id=1, replica_groups=mesh['seq'=16,'batch'=2] {'batch','seq'}, dimensions={0} | all-to-all | bytes 2097152 | tf_op jit(solution)/shard_map/all_to_all | solution.py:427
  39.1 12.3 %forward.1 = (bf16[32,2,32,256]{3,2,1,0:T(8,128)(2,1)}, f32[17,2,64,256]{3,2,1,0:T(8,128)}) custom-call(bf16[2,16,64,256]{3,2,1,0:T(8,128)(2,1)} %bitcast.13, f32[17,2,256]{2,1,0:T(2,128)} %constant.16.clone.twist_ref, bf16[2,512,512]{2,1,0:T(8,128)(2,1)} %constant.17.clone.matrix_ref), custom_call_target="tpu_custom_call" | custom-call | tf_op jit(solution)/shard_map/forward/pallas_call | solution.py:212
  51.5 3.7 %all-to-all-start.1 = ((bf16[16,2,2,32,256]{4,3,2,1,0:T(8,128)(2,1)}), bf16[16,2,2,32,256]{4,3,2,1,0:T(8,128)(2,1)S(1)}, u32[]{:S(2)}, u32[]{:S(2)}) async-start(bf16[16,2,2,32,256]{4,3,2,1,0:T(8,128)(2,1)} %bitcast.18), calls=%async_computation.1 | async-start | bytes 2097152 | tf_op jit(solution)/shard_map/all_to_all | solution.py:434
  55.1 0.5 compare_convert_fusion.flip_ref
  55.6 22.3 %all-to-all-done.1.grad_ref = bf16[16,2,2,32,256]{4,3,2,1,0:T(8,128)(2,1)S(1)} async-done(((bf16[16,2,2,32,256]{4,3,2,1,0:T(8,128)(2,1)}), bf16[16,2,2,32,256]{4,3,2,1,0:T(8,128)(2,1)S(1)}, u32[]{:S(2)}, u32[]{:S(2)}) %all-to-all-start.1) | async-done | bytes 1048608 | tf_op jit(solution)/shard_map/all_to_all | solution.py:434
  78.0 0.0 copy-start
  78.0 1.0 copy-done
  79.0 8.9 %update.1 = (f32[2,2,256,512]{3,2,1,0:T(8,128)}, f32[2,2,256,512]{3,2,1,0:T(8,128)}, f32[2,2,256,512]{3,2,1,0:T(8,128)}, bf16[16,2,2,32,256]{4,3,2,1,0:T(8,128)(2,1)}) custom-call(s32[2]{0:T(128)} %compare_convert_fusion.flip_ref, bf16[16,2,2,32,256]{4,3,2,1,0:T(8,128)(2,1)} %copy-done, f32[2,2,256,512]{3,2,1,0:T(8,128)} %spec_ref.1, ...), custom_call_target="tpu_custom_call" | custom-call | tf_op jit(solution)/shard_map/update/pallas_call | solution.py:260
  87.9 31.5 %all_to_all.21 = bf16[16,2,2,32,256]{4,3,2,1,0:T(8,128)(2,1)} all-to-all(bf16[16,2,2,32,256]{4,3,2,1,0:T(8,128)(2,1)} %get-tuple-element.15), channel_id=1, replica_groups=mesh['seq'=16,'batch'=2] {'seq'}, dimensions={0} | all-to-all | bytes 2097152 | tf_op jit(solution)/shard_map/all_to_all | solution.py:440
  119.4 13.1 %inverse.1 = bf16[2,16,32,256]{3,2,1,0:T(8,128)(2,1)} custom-call(f32[17,2,64,256]{3,2,1,0:T(8,128)} %get-tuple-element.14.spectra_ref, bf16[32,2,32,256]{3,2,1,0:T(8,128)(2,1)} %bitcast.15, f32[17,2,256]{2,1,0:T(2,128)} %constant.16.clone.twist_ref, bf16[2,512,512]{2,1,0:T(8,128)(2,1)} %constant.18.clone.matrix_ref), custom_call_target="tpu_custom_call" | custom-call | tf_op jit(solution)/shard_map/inverse/pallas_call | solution.py:321
  132.6 20.3 %all_to_all.22 = bf16[32,1,32,256]{3,2,1,0:T(8,128)(2,1)} all-to-all(bf16[32,1,32,256]{3,2,1,0:T(8,128)(2,1)} %bitcast.16), channel_id=1, replica_groups=mesh['seq'=16,'batch'=2] {'batch','seq'}, dimensions={0} | all-to-all | bytes 1048576 | tf_op jit(solution)/shard_map/all_to_all | solution.py:446
  152.9 3.6 %unpack.1 = bf16[256,1024]{1,0:T(8,128)(2,1)} custom-call(bf16[1024,256]{1,0:T(8,128)(2,1)} %bitcast.17), custom_call_target="tpu_custom_call" | custom-call | tf_op jit(solution)/shard_map/unpack/pallas_call | solution.py:141
Async XLA Ops:
  51.5 26.5 %all-to-all-start.1 = ((bf16[16,2,2,32,256]{4,3,2,1,0:T(8,128)(2,1)}), bf16[16,2,2,32,256]{4,3,2,1,0:T(8,128)(2,1)S(1)}, u32[]{:S(2)}, u32[]{:S(2)}) async-start(bf16[16,2,2,32,256]{4,3,2,1,0:T(8,128)(2,1)} %bitcast.18), calls=%async_computation.1 | async-start | bytes 2097152 | tf_op jit(solution)/shard_map/all_to_all | solution.py:434
  78.0 1.0 copy-start

commit v2 on v1

v2 whole, which is shorter than its diff:
```python
import functools
import math

import jax
import jax.numpy as jnp
import numpy as np
from jax import lax
from jax.experimental import pallas as pl
from jax.experimental.pallas import tpu as pltpu
from jax.sharding import PartitionSpec as P

step_rate = 0.5
epsilon = 1e-06
sub = 16
lane = 128


def turn_table(numer, modulus):
    phase = 2.0 * math.pi * (numer % modulus) / modulus
    return np.cos(phase), np.sin(phase)


def twist_table(outer, points):
    half = outer // 2
    index = np.arange(half + 1)[:, None] * np.arange(points)[None, :]
    cos, sin = turn_table(index, outer * points)
    return np.stack([cos, sin], axis=1).astype(np.float32)


def point_matrices(points, scale_back):
    index = np.arange(points)[:, None] * np.arange(points)[None, :]
    cos, sin = turn_table(index, points)
    ahead = np.block([[cos, -sin], [sin, cos]])
    back = np.block([[cos, sin], [-sin, cos]]) * scale_back
    return ahead.astype(np.float32), back.astype(np.float32)


def times_phase(re, im, turns, count):
    if turns == 0:
        return re, im
    if 4 * turns == count:
        return im, -re
    cos = math.cos(2.0 * math.pi * turns / count)
    sin = math.sin(2.0 * math.pi * turns / count)
    return re * cos + im * sin, im * cos - re * sin


def half_spectrum(values):
    total = 2 * len(values)
    if total == 2:
        return [(values[0], None), (values[0], None)]
    even = half_spectrum(values[0::2])
    odd = half_spectrum(values[1::2])
    quarter = total // 4
    out = [None] * (total // 2 + 1)
    for index in range(quarter + 1):
        even_re, even_im = even[index]
        odd_re, odd_im = odd[index]
        if index == 0:
            out[0] = (even_re + odd_re, None)
            out[total // 2] = (even_re - odd_re, None)
        elif index == quarter:
            out[index] = (even_re, -odd_re)
        else:
            turned_re, turned_im = times_phase(odd_re, odd_im, index, total)
            out[index] = (even_re + turned_re, even_im + turned_im)
            out[total // 2 - index] = (even_re - turned_re, turned_im - even_im)
    return out


def real_segments(bins):
    count = 2 * (len(bins) - 1)
    if count == 2:
        return [bins[0][0] + bins[1][0]]
    quarter = count // 4
    even = [None] * (quarter + 1)
    odd = [None] * (quarter + 1)
    for index in range(quarter + 1):
        low_re, low_im = bins[index]
        high_re, high_im = bins[count // 2 - index]
        if index == 0:
            even[0] = (low_re + high_re, None)
            odd[0] = (low_re - high_re, None)
        elif index == quarter:
            even[index] = (low_re, None)
            odd[index] = (-low_im, None)
        else:
            even[index] = (low_re + high_re, low_im - high_im)
            diff_re, diff_im = low_re - high_re, low_im + high_im
            cos = math.cos(2.0 * math.pi * index / count)
            sin = math.sin(2.0 * math.pi * index / count)
            odd[index] = (diff_re * cos - diff_im * sin, diff_re * sin + diff_im * cos)
    first = real_segments(even)
    second = real_segments(odd)
    return [item for pair in zip(first, second) for item in pair]


both_last = (((1,), (1,)), ((), ()))
both_first = (((0,), (0,)), ((), ()))


def square_eye(points, flipped):
    row = lax.broadcasted_iota(jnp.int32, (points, points), 0)
    col = lax.broadcasted_iota(jnp.int32, (points, points), 1)
    picked = jnp.where(flipped, points - 1 - col, col)
    return jnp.where(row == picked, 1.0, 0.0).astype(jnp.bfloat16)


whole = pl.BlockSpec(memory_space=pltpu.VMEM)
roomy = pltpu.CompilerParams(vmem_limit_bytes=24 << 20)


def pack_kernel(signal_ref, cotangent_ref, out_ref, *, narrow, width):
    points, channels = signal_ref.shape
    for part, source in enumerate((signal_ref, cotangent_ref)):
        for left in range(0, channels, width):
            turned = source[:, left : left + width].T.reshape(width // narrow, narrow, points)
            first = left // narrow
            out_ref[first : first + width // narrow, part * narrow : (part + 1) * narrow, :] = turned


def pack_call(signal, cotangent, narrow):
    points, channels = signal.shape
    return pl.pallas_call(
        functools.partial(pack_kernel, narrow=narrow, width=math.gcd(channels, 256)),
        in_specs=[whole, whole],
        out_specs=whole,
        out_shape=jax.ShapeDtypeStruct((channels // narrow, 2 * narrow, points), jnp.bfloat16),
        compiler_params=roomy,
        name="pack",
    )(signal, cotangent)


def unpack_kernel(in_ref, out_ref):
    out_ref[...] = in_ref[...].T


def unpack_call(rows):
    channels, points = rows.shape
    width = math.gcd(channels, 512)
    return pl.pallas_call(
        unpack_kernel,
        grid=(channels // width,),
        in_specs=[pl.BlockSpec((width, points), lambda step: (step, 0))],
        out_specs=pl.BlockSpec((points, width), lambda step: (0, step)),
        out_shape=jax.ShapeDtypeStruct((points, channels), jnp.bfloat16),
        compiler_params=roomy,
        name="unpack",
    )(rows)


def over_chunks(emit, segments, chunk):
    emit(0, 1, False)
    emit(segments, 1, False)
    count = (segments - 1) // chunk

    def step(index, carry):
        emit(1 + index * chunk, chunk, True)
        return carry

    lax.fori_loop(0, count, step, 0)
    if (segments - 1) % chunk:
        emit(1 + count * chunk, (segments - 1) % chunk, True)


def split_dot(values, matrices):
    first = jnp.dot(values, matrices[0], preferred_element_type=jnp.float32)
    return first + jnp.dot(values, matrices[1], preferred_element_type=jnp.float32)


def forward_kernel(in_ref, twist_ref, matrix_ref, grad_ref, spectra_ref, mid_ref, *, scale, chunk):
    sequences, segments, pair_rows, points = in_ref.shape
    narrow = pair_rows // 2
    rows = sequences * narrow
    tiles = pair_rows // sub

    def tile_step(step, carry):
        which = step // tiles
        piece = step % tiles
        start = pl.multiple_of(piece * sub, sub)
        target = (piece // (tiles // 2)) * rows + which * narrow
        target = pl.multiple_of(target + (piece % (tiles // 2)) * sub, sub)
        for left in range(0, points, lane):
            here = slice(left, left + lane)
            after = slice(points + left, points + left + lane)
            values = [
                in_ref[which, seg, pl.ds(start, sub), here].astype(jnp.float32) for seg in range(segments)
            ]
            for index, (re, im) in enumerate(half_spectrum(values)):
                cos = twist_ref[index, 0:1, here]
                sin = twist_ref[index, 1:2, here]
                if im is None:
                    new_re, new_im = re * cos, -(re * sin)
                else:
                    new_re, new_im = re * cos + im * sin, im * cos - re * sin
                mid_ref[index, pl.ds(target, sub), here] = new_re.astype(jnp.bfloat16)
                mid_ref[index, pl.ds(target, sub), after] = new_im.astype(jnp.bfloat16)
        return carry

    lax.fori_loop(0, sequences * tiles, tile_step, 0)

    def emit(base, count, paired):
        values = mid_ref[pl.ds(base, count)].reshape(count * 2 * rows, 2 * points)
        full = split_dot(values, matrix_ref).reshape(count, 2 * rows, 2 * points)
        for extra in range(count):
            residue = base + extra
            signal_re, signal_im = full[extra, :rows, :points], full[extra, :rows, points:]
            cotan_re, cotan_im = full[extra, rows:, :points], full[extra, rows:, points:]
            spectra_ref[residue, 0] = signal_re
            spectra_ref[residue, 1] = signal_im
            real_term = signal_re * cotan_re + signal_im * cotan_im
            imag_term = signal_re * cotan_im - signal_im * cotan_re
            real_sum = jnp.sum(real_term.reshape(sequences, narrow, points), axis=0) * scale
            imag_sum = jnp.sum(imag_term.reshape(sequences, narrow, points), axis=0) * scale
            grad_ref[residue, 0] = real_sum.astype(jnp.bfloat16)
            grad_ref[residue, 1] = imag_sum.astype(jnp.bfloat16)
            if paired:
                grad_ref[2 * segments - residue, 0] = real_sum.astype(jnp.bfloat16)
                grad_ref[2 * segments - residue, 1] = (-imag_sum).astype(jnp.bfloat16)

    over_chunks(emit, segments, chunk)


def forward_call(arrived, twist, matrices):
    sequences, segments, pair_rows, points = arrived.shape
    narrow = pair_rows // 2
    outer = 2 * segments
    rows = sequences * narrow
    return pl.pallas_call(
        functools.partial(forward_kernel, scale=1.0 / (outer * points), chunk=5),
        in_specs=[whole, whole, whole],
        out_specs=[whole, whole],
        out_shape=[
            jax.ShapeDtypeStruct((outer, 2, narrow, points), jnp.bfloat16),
            jax.ShapeDtypeStruct((segments + 1, 2, rows, points), jnp.float32),
        ],
        scratch_shapes=[pltpu.VMEM((segments + 1, 2 * rows, 2 * points), jnp.bfloat16)],
        compiler_params=roomy,
        name="forward",
    )(arrived, twist, matrices)


def moved(grad, spec, first, second):
    new_first = 0.9 * first + 0.1 * grad
    new_second = 0.99 * second + 0.01 * grad * grad
    return spec - step_rate * jnp.tanh(new_first / (jnp.sqrt(new_second) + epsilon)), new_first, new_second


def filter_kernel(flip_ref, grad_ref, spec_ref, first_ref, second_ref, out_ref):
    _, local_outer, points, width = spec_ref.shape
    for row in range(local_outer):
        eye = square_eye(points, flip_ref[row] > 0)
        for part in range(2):
            sent = grad_ref[:, row, part].reshape(width, points)
            grad = lax.dot_general(eye, sent, both_last, preferred_element_type=jnp.float32)
            new_spec, _, _ = moved(grad, spec_ref[part, row], first_ref[part, row], second_ref[part, row])
            turned = lax.dot_general(
                new_spec.astype(jnp.bfloat16), eye, both_first, preferred_element_type=jnp.float32
            )
            out_ref[:, row, part] = turned.astype(jnp.bfloat16).reshape(grad_ref.shape[0], -1, points)


def filter_call(flips, sent, spectrum, first_moment, second_moment):
    return pl.pallas_call(
        filter_kernel,
        in_specs=[pl.BlockSpec(memory_space=pltpu.SMEM), whole, whole, whole, whole],
        out_specs=whole,
        out_shape=jax.ShapeDtypeStruct(sent.shape, jnp.bfloat16),
        compiler_params=roomy,
        name="filter",
    )(flips, sent, spectrum, first_moment, second_moment)


def update_kernel(
    flip_ref, grad_ref, spec_ref, first_ref, second_ref, new_spec_ref, new_first_ref, new_second_ref
):
    points, width = spec_ref.shape[2:]
    eye = square_eye(points, flip_ref[pl.program_id(0)] > 0)
    for part in range(2):
        sent = grad_ref[:, 0, part].reshape(width, points)
        grad = lax.dot_general(eye, sent, both_last, preferred_element_type=jnp.float32)
        new_spec, new_first, new_second = moved(
            grad, spec_ref[part, 0], first_ref[part, 0], second_ref[part, 0]
        )
        new_spec_ref[part, 0] = new_spec
        new_first_ref[part, 0] = new_first
        new_second_ref[part, 0] = new_second


def update_call(flips, sent, spectrum, first_moment, second_moment):
    groups, local_outer, _, narrow, points = sent.shape
    channels = spectrum.shape[3]
    state = pl.BlockSpec((2, 1, points, channels), lambda row, flags: (0, row, 0, 0))
    wire = pl.BlockSpec((groups, 1, 2, narrow, points), lambda row, flags: (0, row, 0, 0, 0))
    return pl.pallas_call(
        update_kernel,
        grid_spec=pltpu.PrefetchScalarGridSpec(
            num_scalar_prefetch=1,
            grid=(local_outer,),
            in_specs=[wire, state, state, state],
            out_specs=[state, state, state],
        ),
        out_shape=[jax.ShapeDtypeStruct(spectrum.shape, jnp.float32)] * 3,
        compiler_params=roomy,
        name="update",
    )(flips, sent, spectrum, first_moment, second_moment)


def inverse_kernel(spectra_ref, filter_ref, twist_ref, matrix_ref, out_ref, mid_ref, *, chunk):
    sequences, segments, narrow, points = out_ref.shape
    rows = sequences * narrow

    def mixed(residue, paired):
        filter_re = filter_ref[residue, 0].astype(jnp.float32)
        filter_im = filter_ref[residue, 1].astype(jnp.float32)
        if paired:
            filter_re = filter_re + filter_ref[2 * segments - residue, 0].astype(jnp.float32)
            filter_im = filter_im - filter_ref[2 * segments - residue, 1].astype(jnp.float32)
        signal_re = spectra_ref[residue, 0].reshape(sequences, narrow, points)
        signal_im = spectra_ref[residue, 1].reshape(sequences, narrow, points)
        mixed_re = (signal_re * filter_re - signal_im * filter_im).reshape(rows, points)
        mixed_im = (signal_re * filter_im + signal_im * filter_re).reshape(rows, points)
        return jnp.concatenate([mixed_re.astype(jnp.bfloat16), mixed_im.astype(jnp.bfloat16)], axis=1)

    def emit(base, count, paired):
        values = jnp.concatenate([mixed(base + extra, paired) for extra in range(count)], axis=0)
        full = split_dot(values, matrix_ref).reshape(count, rows, 2 * points)
        for extra in range(count):
            residue = base + extra
            cos = twist_ref[residue, 0:1]
            sin = twist_ref[residue, 1:2]
            mid_ref[residue, 0] = full[extra, :, :points] * cos - full[extra, :, points:] * sin
            mid_ref[residue, 1] = full[extra, :, :points] * sin + full[extra, :, points:] * cos

    over_chunks(emit, segments, chunk)
    tiles = narrow // sub

    def tile_step(step, carry):
        which = step // tiles
        start = pl.multiple_of((step % tiles) * sub, sub)
        source = pl.multiple_of(step * sub, sub)
        for left in range(0, points, lane):
            here = slice(left, left + lane)
            bins = [
                tuple(mid_ref[index, part, pl.ds(source, sub), here] for part in range(2))
                for index in range(segments + 1)
            ]
            for seg, value in enumerate(real_segments(bins)):
                out_ref[which, seg, pl.ds(start, sub), here] = value.astype(jnp.bfloat16)
        return carry

    lax.fori_loop(0, sequences * tiles, tile_step, 0)


def inverse_call(spectra, filters, twist, matrices):
    residues, _, rows, points = spectra.shape
    segments = residues - 1
    narrow = filters.shape[2]
    sequences = rows // narrow
    return pl.pallas_call(
        functools.partial(inverse_kernel, chunk=5),
        in_specs=[whole, whole, whole, whole],
        out_specs=whole,
        out_shape=jax.ShapeDtypeStruct((sequences, segments, narrow, points), jnp.bfloat16),
        scratch_shapes=[pltpu.VMEM((residues, 2, rows, points), jnp.float32)],
        compiler_params=roomy,
        name="inverse",
    )(spectra, filters, twist, matrices)


def pack_plain(signal, cotangent, narrow):
    points, channels = signal.shape
    both = jnp.stack([signal, cotangent]).reshape(2, points, channels // narrow, narrow)
    return both.transpose(2, 0, 3, 1).reshape(channels // narrow, 2 * narrow, points)


def forward_plain(arrived, twist, matrices):
    sequences, segments, pair_rows, points = arrived.shape
    narrow = pair_rows // 2
    rows = sequences * narrow
    parts = arrived.reshape(sequences, segments, 2, narrow, points).astype(jnp.float32)
    parts = parts.transpose(1, 2, 0, 3, 4).reshape(segments, 2 * rows, points)
    bins = half_spectrum([parts[seg] for seg in range(segments)])
    re = jnp.stack([item[0] for item in bins])
    im = jnp.stack([jnp.zeros_like(item[0]) if item[1] is None else item[1] for item in bins])
    cos, sin = twist[:, 0][:, None], twist[:, 1][:, None]
    mid = jnp.concatenate([re * cos + im * sin, im * cos - re * sin], axis=2).astype(jnp.bfloat16)
    full = split_dot(mid, matrices)
    signal_re, signal_im = full[:, :rows, :points], full[:, :rows, points:]
    cotan_re, cotan_im = full[:, rows:, :points], full[:, rows:, points:]
    shape = (segments + 1, sequences, narrow, points)
    scale = 1.0 / (2 * segments * points)
    real = jnp.sum((signal_re * cotan_re + signal_im * cotan_im).reshape(shape), axis=1) * scale
    imag = jnp.sum((signal_re * cotan_im - signal_im * cotan_re).reshape(shape), axis=1) * scale
    real = jnp.concatenate([real, real[1:segments][::-1]])
    imag = jnp.concatenate([imag, -imag[1:segments][::-1]])
    grad = jnp.stack([real, imag], axis=1).astype(jnp.bfloat16)
    return grad, jnp.stack([signal_re, signal_im], axis=1)


def gradient_plain(flips, sent, shape):
    arrived = sent.astype(jnp.float32).transpose(2, 1, 4, 0, 3).reshape(shape)
    return jnp.where((flips > 0)[None, :, None, None], arrived[:, :, ::-1], arrived)


def filter_plain(flips, sent, spectrum, first_moment, second_moment):
    groups, local_outer, _, narrow, points = sent.shape
    grad = gradient_plain(flips, sent, spectrum.shape)
    new_spec, _, _ = moved(grad, spectrum, first_moment, second_moment)
    out = jnp.where((flips > 0)[None, :, None, None], new_spec[:, :, ::-1], new_spec).astype(jnp.bfloat16)
    return out.reshape(2, local_outer, points, groups, narrow).transpose(3, 1, 0, 4, 2)


def update_plain(flips, sent, spectrum, first_moment, second_moment):
    return moved(gradient_plain(flips, sent, spectrum.shape), spectrum, first_moment, second_moment)


def inverse_plain(spectra, filters, twist, matrices):
    residues, _, rows, points = spectra.shape
    segments = residues - 1
    narrow = filters.shape[2]
    sequences = rows // narrow
    wide = filters.astype(jnp.float32)
    mirrored = jnp.concatenate([jnp.zeros_like(wide[:1]), wide[segments + 1 :][::-1], jnp.zeros_like(wide[:1])])
    filter_re = (wide[: segments + 1, 0] + mirrored[:, 0])[:, None]
    filter_im = (wide[: segments + 1, 1] - mirrored[:, 1])[:, None]
    shape = (residues, sequences, narrow, points)
    signal_re, signal_im = spectra[:, 0].reshape(shape), spectra[:, 1].reshape(shape)
    mixed_re = (signal_re * filter_re - signal_im * filter_im).reshape(residues, rows, points)
    mixed_im = (signal_re * filter_im + signal_im * filter_re).reshape(residues, rows, points)
    full = split_dot(jnp.concatenate([mixed_re, mixed_im], axis=2).astype(jnp.bfloat16), matrices)
    cos, sin = twist[:, 0][:, None], twist[:, 1][:, None]
    mid_re = full[..., :points] * cos - full[..., points:] * sin
    mid_im = full[..., :points] * sin + full[..., points:] * cos
    out = jnp.stack(real_segments([(mid_re[index], mid_im[index]) for index in range(residues)]))
    out = out.reshape(segments, sequences, narrow, points).transpose(1, 0, 2, 3)
    return out.astype(jnp.bfloat16)


def high_low(matrix):
    high = matrix.astype(jnp.bfloat16)
    low = (matrix - high.astype(np.float32)).astype(jnp.bfloat16)
    return np.stack([high, low])


def per_device(inputs, grad_out, spectrum, first_moment, second_moment):
    seq_count = lax.axis_size("seq")
    batch_count = lax.axis_size("batch")
    batch_rows, points, channels = inputs.shape
    narrow = channels // (seq_count * batch_count)
    local_outer = spectrum.shape[1]
    outer = 2 * seq_count
    tiled = narrow % sub == 0 and points % lane == 0 and batch_rows == 1
    twist = jnp.asarray(twist_table(outer, points))
    ahead, back = point_matrices(points, 1.0 / (outer * points))
    ahead, back = jnp.asarray(high_low(ahead)), jnp.asarray(high_low(back))

    pack = pack_call if tiled else pack_plain
    packed = jnp.stack([pack(inputs[row], grad_out[row], narrow) for row in range(batch_rows)], axis=1)
    arrived = lax.all_to_all(packed, ("batch", "seq"), split_axis=0, concat_axis=0, tiled=True)
    arrived = arrived.reshape(batch_count, seq_count, batch_rows, 2 * narrow, points)
    arrived = arrived.transpose(0, 2, 1, 3, 4).reshape(-1, seq_count, 2 * narrow, points)
    sequences = arrived.shape[0]

    grad, spectra = (forward_call if tiled else forward_plain)(arrived, twist, ahead)
    grad = grad.reshape(seq_count, local_outer, 2, narrow, points)
    sent = lax.all_to_all(grad, "seq", split_axis=0, concat_axis=0, tiled=True)

    residues = lax.axis_index("seq") * local_outer + jnp.arange(local_outer, dtype=jnp.int32)
    flips = (residues > seq_count).astype(jnp.int32)
    states = (spectrum, first_moment, second_moment)
    filters = (filter_call if tiled else filter_plain)(flips, sent, *states)
    filters = lax.all_to_all(filters, "seq", split_axis=0, concat_axis=0, tiled=True)
    new_spectrum, new_first, new_second = (update_call if tiled else update_plain)(flips, sent, *states)
    filters = filters.reshape(outer, 2, narrow, points)

    rows = (inverse_call if tiled else inverse_plain)(spectra, filters, twist, back)
    rows = rows.reshape(batch_count, batch_rows, seq_count, narrow, points).transpose(0, 2, 1, 3, 4)
    rows = rows.reshape(batch_count * seq_count, batch_rows, narrow, points)
    rows = lax.all_to_all(rows, ("batch", "seq"), split_axis=0, concat_axis=0, tiled=True)
    if tiled:
        filtered = unpack_call(rows.reshape(channels, points))[None]
    else:
        filtered = rows.transpose(1, 3, 0, 2).reshape(batch_rows, points, channels)
    return new_spectrum, new_first, new_second, filtered


def solution(mesh):
    return jax.shard_map(
        per_device,
        mesh=mesh,
        in_specs=(
            P("batch", "seq", None),
            P("batch", "seq", None),
            P(None, "seq", None, "batch"),
            P(None, "seq", None, "batch"),
            P(None, "seq", None, "batch"),
        ),
        out_specs=(
            P(None, "seq", None, "batch"),
            P(None, "seq", None, "batch"),
            P(None, "seq", None, "batch"),
            P("batch", "seq", None),
        ),
        check_vma=False,
    )
```

time: 157 us -> 134 us (0.85)
  Pallas kernels: 41.9 us -> 16.7 us
  blocking collectives: 86.4 us -> 65.7 us
  local copies, waits for them, and re-layouts: 1 us -> 11.6 us
  waiting for transfers between devices: 22.3 us -> 30.9 us
  starting transfers between devices: 3.66 us -> 8.1 us
    all_to_all x1 -> x0, blocking collectives: 20.3 us -> none  [per_device(): lax.all_to_all(rows, ('batch', 'seq'), split_axis=0, concat_axis=0, tiled...]
    pallas_call x2 -> x3, Pallas kernels: 17.1 us -> 5.49 us  [the longest x1 2.75 us: inverse_call(): pl.pallas_call(functools.partial(inverse_kernel, chunk=5), in_specs=[whol...]
    unnamed x2 -> x28, local copies, waits for them, and re-layouts: 1 us -> 11.6 us
    all_to_all x0 -> x1, waiting for transfers between devices: none -> 8.06 us  [per_device(): lax.all_to_all(rows, ('batch', 'seq'), split_axis=0, concat_axis=0, tiled...]
    pallas_call x1, Pallas kernels: 12.3 us -> 4.68 us  [forward_call(): pl.pallas_call(functools.partial(forward_kernel, scale=1.0 / (outer * poi...]
    all_to_all x0 -> x1, starting transfers between devices: none -> 4.45 us  [per_device(): lax.all_to_all(rows, ('batch', 'seq'), split_axis=0, concat_axis=0, tiled...]
    pallas_call x1, Pallas kernels: 8.94 us -> 4.62 us  [update_call(): pl.pallas_call(update_kernel, grid_spec=pltpu.PrefetchScalarGridSpec(num_...]
    pallas_call x1, Pallas kernels: 3.58 us -> 1.91 us  [unpack_call(): pl.pallas_call(unpack_kernel, grid=(channels // width,), in_specs=[pl.Blo...]
  transfers between devices with their start and end apart: 1 -> 2, of which waited for: 1 -> 2; matrix products, arithmetic and copies ran while one was open for 0% -> 0% of each run, Pallas kernels for 0% -> 3%
where the time goes in v2:
time: 134 us
  blocking collectives  65.7 us (49%)
  waiting for transfers between devices  30.9 us (23%)
  Pallas kernels  16.7 us (12%)
  local copies, waits for them, and re-layouts  11.6 us (9%)
  starting transfers between devices  8.1 us (6%)
    all_to_all x1, blocking collectives, per_device(): lax.all_to_all(packed, ('batch', 'seq'), split_axis=0, concat_axis=0, til...  34.3 us
    all_to_all x1, blocking collectives, per_device(): lax.all_to_all(filters, 'seq', split_axis=0, concat_axis=0, tiled=True)  31.4 us
    all_to_all x1, waiting for transfers between devices, per_device(): sent = lax.all_to_all(grad, 'seq', split_axis=0, concat_axis=0, tiled=True)  22.8 us
    unnamed x28, local copies, waits for them, and re-layouts  11.6 us
    all_to_all x1, waiting for transfers between devices, per_device(): lax.all_to_all(rows, ('batch', 'seq'), split_axis=0, concat_axis=0, tiled...  8.06 us
    pallas_call x1, Pallas kernels, forward_call(): pl.pallas_call(functools.partial(forward_kernel, scale=1.0 / (outer * poi...  4.68 us
    pallas_call x1, Pallas kernels, update_call(): pl.pallas_call(update_kernel, grid_spec=pltpu.PrefetchScalarGridSpec(num_...  4.62 us
    all_to_all x1, starting transfers between devices, per_device(): lax.all_to_all(rows, ('batch', 'seq'), split_axis=0, concat_axis=0, tiled...  4.45 us
  transfers between devices with their start and end apart: 2, of which 2 were waited for; matrix products, arithmetic and copies ran while one was open for 0% of the time, Pallas kernels for 3%

profile of v2, /device:TPU:0, one launch (start us, length us, event | category | flops | bytes accessed | tf_op | source)
XLA Modules:
  0.0 133.7 jit_solution(6123245287668904059)
XLA Ops:
  0.6 0.0 copy-start.11
  0.6 1.0 copy-done.11
  1.7 0.0 copy-start.12
  1.7 1.0 copy-done.12
  2.7 0.3 pack.1
  3.0 34.3 %all_to_all.20 = bf16[32,1,64,256]{3,2,1,0:T(8,128)(2,1)S(1)} all-to-all(bf16[32,1,64,256]{3,2,1,0:T(8,128)(2,1)S(1)} %bitcast.14), channel_id=1, replica_groups=mesh['seq'=16,'batch'=2] {'batch','seq'}, dimensions={0} | all-to-all | bytes 2097152 | tf_op jit(solution)/shard_map/all_to_all | solution.py:460
  37.4 0.0 copy-done.8
  37.4 0.0 copy-done.13
  37.4 4.7 %forward.1 = (bf16[32,2,32,256]{3,2,1,0:T(8,128)(2,1)S(1)}, f32[17,2,64,256]{3,2,1,0:T(8,128)S(1)}) custom-call(bf16[2,16,64,256]{3,2,1,0:T(8,128)(2,1)S(1)} %bitcast.13, f32[17,2,256]{2,1,0:T(2,128)S(1)} %copy-done.13, bf16[2,512,512]{2,1,0:T(8,128)(2,1)S(1)} %copy-done.8), custom_call_target="tpu_custom_call" | custom-call | tf_op jit(solution)/shard_map/forward/pallas_call | solution.py:229
  42.0 0.0 copy-start.5
  42.1 1.4 %copy-done.5 = f32[17,2,64,256]{3,2,1,0:T(8,128)} copy-done((f32[17,2,64,256]{3,2,1,0:T(8,128)}, f32[17,2,64,256]{3,2,1,0:T(8,128)S(1)}, u32[]{:S(2)}) %copy-start.5) | copy-done | bytes 2228248
  43.4 1.0 copy-done.9
  44.4 3.7 %all-to-all-start.1 = ((bf16[16,2,2,32,256]{4,3,2,1,0:T(8,128)(2,1)}), bf16[16,2,2,32,256]{4,3,2,1,0:T(8,128)(2,1)S(1)}, u32[]{:S(2)}, u32[]{:S(2)}) async-start(bf16[16,2,2,32,256]{4,3,2,1,0:T(8,128)(2,1)} %bitcast.17), calls=%async_computation.1 | async-start | bytes 2097152 | tf_op jit(solution)/shard_map/all_to_all | solution.py:467
  48.1 22.8 %all-to-all-done.1.grad_ref = bf16[16,2,2,32,256]{4,3,2,1,0:T(8,128)(2,1)S(1)} async-done(((bf16[16,2,2,32,256]{4,3,2,1,0:T(8,128)(2,1)}), bf16[16,2,2,32,256]{4,3,2,1,0:T(8,128)(2,1)S(1)}, u32[]{:S(2)}, u32[]{:S(2)}) %all-to-all-start.1) | async-done | bytes 1048608 | tf_op jit(solution)/shard_map/all_to_all | solution.py:467
  70.9 0.0 copy-done
  70.9 1.6 %copy-done.1 = f32[2,2,256,512]{3,2,1,0:T(8,128)S(1)} copy-done((f32[2,2,256,512]{3,2,1,0:T(8,128)S(1)}, f32[2,2,256,512]{3,2,1,0:T(8,128)}, u32[]{:S(2)}) %copy-start.1) | copy-done | bytes 2097176
  72.5 1.6 %copy-done.3 = f32[2,2,256,512]{3,2,1,0:T(8,128)S(1)} copy-done((f32[2,2,256,512]{3,2,1,0:T(8,128)S(1)}, f32[2,2,256,512]{3,2,1,0:T(8,128)}, u32[]{:S(2)}) %copy-start.3) | copy-done | bytes 2097176
  74.1 2.4 %filter.1 = bf16[16,2,2,32,256]{4,3,2,1,0:T(8,128)(2,1)S(1)} custom-call(s32[2]{0:T(128)S(1)} %compare_convert_fusion.flip_ref, bf16[16,2,2,32,256]{4,3,2,1,0:T(8,128)(2,1)S(1)} %all-to-all-done.1.grad_ref, f32[2,2,256,512]{3,2,1,0:T(8,128)S(1)} %copy-done, f32[2,2,256,512]{3,2,1,0:T(8,128)S(1)} %copy-done.1, f32[2,2,256,512]{3,2,1,0:T(8,128)S(1)} %copy-done.3), custom_call_target="tpu_custom_call" | custom-call | tf_op jit(solution)/shard_map/filter/pallas_call | solution.py:264
  76.5 0.0 copy-start.10
  76.5 31.4 %all_to_all.21 = bf16[16,2,2,32,256]{4,3,2,1,0:T(8,128)(2,1)S(1)} all-to-all(bf16[16,2,2,32,256]{4,3,2,1,0:T(8,128)(2,1)S(1)} %filter.1), channel_id=1, replica_groups=mesh['seq'=16,'batch'=2] {'seq'}, dimensions={0} | all-to-all | bytes 2097152 | tf_op jit(solution)/shard_map/all_to_all | solution.py:473
  107.9 0.0 copy-done.6
  107.9 0.0 copy-done.10
  107.9 2.8 %inverse.1 = bf16[2,16,32,256]{3,2,1,0:T(8,128)(2,1)S(1)} custom-call(f32[17,2,64,256]{3,2,1,0:T(8,128)S(1)} %copy-done.6, bf16[32,2,32,256]{3,2,1,0:T(8,128)(2,1)S(1)} %bitcast.15, f32[17,2,256]{2,1,0:T(2,128)S(1)} %copy-done.13, bf16[2,512,512]{2,1,0:T(8,128)(2,1)S(1)} %copy-done.10), custom_call_target="tpu_custom_call" | custom-call | tf_op jit(solution)/shard_map/inverse/pallas_call | solution.py:360
  110.7 0.0 copy-start.7
  110.7 0.8 copy-done.7
  111.5 4.4 %all-to-all-start.3 = ((bf16[32,1,32,256]{3,2,1,0:T(8,128)(2,1)}), bf16[32,1,32,256]{3,2,1,0:T(8,128)(2,1)}, u32[]{:S(2)}, u32[]{:S(2)}) async-start(bf16[32,1,32,256]{3,2,1,0:T(8,128)(2,1)} %bitcast.16), calls=%async_computation.3 | async-start | bytes 1048576 | tf_op jit(solution)/shard_map/all_to_all | solution.py:480
  115.9 0.0 copy-start.2
  115.9 1.6 %copy-done.2 = f32[2,2,256,512]{3,2,1,0:T(8,128)S(1)} copy-done((f32[2,2,256,512]{3,2,1,0:T(8,128)S(1)}, f32[2,2,256,512]{3,2,1,0:T(8,128)}, u32[]{:S(2)}) %copy-start.2) | copy-done | bytes 2097176
  117.5 1.6 %copy-done.4 = f32[2,2,256,512]{3,2,1,0:T(8,128)S(1)} copy-done((f32[2,2,256,512]{3,2,1,0:T(8,128)S(1)}, f32[2,2,256,512]{3,2,1,0:T(8,128)}, u32[]{:S(2)}) %copy-start.4) | copy-done | bytes 2097176
  119.1 4.6 %update.1 = (f32[2,2,256,512]{3,2,1,0:T(8,128)}, f32[2,2,256,512]{3,2,1,0:T(8,128)}, f32[2,2,256,512]{3,2,1,0:T(8,128)}) custom-call(s32[2]{0:T(128)S(1)} %compare_convert_fusion.flip_ref, bf16[16,2,2,32,256]{4,3,2,1,0:T(8,128)(2,1)S(1)} %all-to-all-done.1.grad_ref, f32[2,2,256,512]{3,2,1,0:T(8,128)S(1)} %copy-done, f32[2,2,256,512]{3,2,1,0:T(8,128)S(1)} %copy-done.2, ...), custom_call_target="tpu_custom_call" | custom-call | tf_op jit(solution)/shard_map/update/pallas_call | solution.py:295
  123.7 8.1 %all-to-all-done.3 = bf16[32,1,32,256]{3,2,1,0:T(8,128)(2,1)} async-done(((bf16[32,1,32,256]{3,2,1,0:T(8,128)(2,1)}), bf16[32,1,32,256]{3,2,1,0:T(8,128)(2,1)}, u32[]{:S(2)}, u32[]{:S(2)}) %all-to-all-start.3) | async-done | bytes 524320 | tf_op jit(solution)/shard_map/all_to_all | solution.py:480
  131.8 1.9 %unpack.1 = bf16[256,1024]{1,0:T(8,128)(2,1)} custom-call(bf16[1024,256]{1,0:T(8,128)(2,1)} %bitcast.9.in_ref), custom_call_target="tpu_custom_call" | custom-call | tf_op jit(solution)/shard_map/unpack/pallas_call | solution.py:141
  (9 shorter events, 0.0 us)
Async XLA Ops:
  0.6 1.0 copy-start.11
  1.7 1.0 copy-start.12
  2.7 34.6 %copy-start.8 = (bf16[2,512,512]{2,1,0:T(8,128)(2,1)S(1)}, bf16[2,512,512]{2,1,0:T(8,128)(2,1)}, u32[]{:S(2)}) copy-start(bf16[2,512,512]{2,1,0:T(8,128)(2,1)} %constant.17.clone.matrix_ref) | copy-start | bytes 3145732
  2.7 34.6 %copy-start.13 = (f32[17,2,256]{2,1,0:T(2,128)S(1)}, f32[17,2,256]{2,1,0:T(2,128)}, u32[]{:S(2)}) copy-start(f32[17,2,256]{2,1,0:T(2,128)} %constant.16.clone.twist_ref) | copy-start | bytes 104452
  37.4 33.5 %copy-start = (f32[2,2,256,512]{3,2,1,0:T(8,128)S(1)}, f32[2,2,256,512]{3,2,1,0:T(8,128)}, u32[]{:S(2)}) copy-start(f32[2,2,256,512]{3,2,1,0:T(8,128)} %spec_ref.3) | copy-start | bytes 6291460
  42.0 1.4 %copy-start.5 = (f32[17,2,64,256]{3,2,1,0:T(8,128)}, f32[17,2,64,256]{3,2,1,0:T(8,128)S(1)}, u32[]{:S(2)}) copy-start(f32[17,2,64,256]{3,2,1,0:T(8,128)S(1)} %get-tuple-element.13.spectra_ref) | copy-start | bytes 6684676
  43.4 1.0 copy-start.9
  44.4 26.5 %all-to-all-start.1 = ((bf16[16,2,2,32,256]{4,3,2,1,0:T(8,128)(2,1)}), bf16[16,2,2,32,256]{4,3,2,1,0:T(8,128)(2,1)S(1)}, u32[]{:S(2)}, u32[]{:S(2)}) async-start(bf16[16,2,2,32,256]{4,3,2,1,0:T(8,128)(2,1)} %bitcast.17), calls=%async_computation.1 | async-start | bytes 2097152 | tf_op jit(solution)/shard_map/all_to_all | solution.py:467
  70.9 1.6 %copy-start.1 = (f32[2,2,256,512]{3,2,1,0:T(8,128)S(1)}, f32[2,2,256,512]{3,2,1,0:T(8,128)}, u32[]{:S(2)}) copy-start(f32[2,2,256,512]{3,2,1,0:T(8,128)} %first_ref.3) | copy-start | bytes 6291460
  72.5 1.6 %copy-start.3 = (f32[2,2,256,512]{3,2,1,0:T(8,128)S(1)}, f32[2,2,256,512]{3,2,1,0:T(8,128)}, u32[]{:S(2)}) copy-start(f32[2,2,256,512]{3,2,1,0:T(8,128)} %second_ref.3) | copy-start | bytes 6291460
  74.1 33.8 %copy-start.6 = (f32[17,2,64,256]{3,2,1,0:T(8,128)S(1)}, f32[17,2,64,256]{3,2,1,0:T(8,128)}, u32[]{:S(2)}) copy-start(f32[17,2,64,256]{3,2,1,0:T(8,128)} %copy-done.5) | copy-start | bytes 6684676
  76.5 31.4 %copy-start.10 = (bf16[2,512,512]{2,1,0:T(8,128)(2,1)S(1)}, bf16[2,512,512]{2,1,0:T(8,128)(2,1)}, u32[]{:S(2)}) copy-start(bf16[2,512,512]{2,1,0:T(8,128)(2,1)} %constant.18.clone.matrix_ref) | copy-start | bytes 3145732
  110.7 0.8 copy-start.7
  111.5 20.3 %all-to-all-start.3 = ((bf16[32,1,32,256]{3,2,1,0:T(8,128)(2,1)}), bf16[32,1,32,256]{3,2,1,0:T(8,128)(2,1)}, u32[]{:S(2)}, u32[]{:S(2)}) async-start(bf16[32,1,32,256]{3,2,1,0:T(8,128)(2,1)} %bitcast.16), calls=%async_computation.3 | async-start | bytes 1048576 | tf_op jit(solution)/shard_map/all_to_all | solution.py:480
  115.9 1.6 %copy-start.2 = (f32[2,2,256,512]{3,2,1,0:T(8,128)S(1)}, f32[2,2,256,512]{3,2,1,0:T(8,128)}, u32[]{:S(2)}) copy-start(f32[2,2,256,512]{3,2,1,0:T(8,128)} %first_ref.3) | copy-start | bytes 6291460
  117.5 1.6 %copy-start.4 = (f32[2,2,256,512]{3,2,1,0:T(8,128)S(1)}, f32[2,2,256,512]{3,2,1,0:T(8,128)}, u32[]{:S(2)}) copy-start(f32[2,2,256,512]{3,2,1,0:T(8,128)} %second_ref.3) | copy-start | bytes 6291460

commit v3 on v2

--- a/solution.py
+++ b/solution.py
@@ -246,10 +246,14 @@
     return spec - step_rate * jnp.tanh(new_first / (jnp.sqrt(new_second) + epsilon)), new_first, new_second
 
 
-def filter_kernel(flip_ref, grad_ref, spec_ref, first_ref, second_ref, out_ref):
+def is_mirrored(row, local_outer):
+    return lax.axis_index("seq") * local_outer + row > lax.axis_size("seq")
+
+
+def filter_kernel(grad_ref, spec_ref, first_ref, second_ref, out_ref):
     _, local_outer, points, width = spec_ref.shape
     for row in range(local_outer):
-        eye = square_eye(points, flip_ref[row] > 0)
+        eye = square_eye(points, is_mirrored(row, local_outer))
         for part in range(2):
             sent = grad_ref[:, row, part].reshape(width, points)
             grad = lax.dot_general(eye, sent, both_last, preferred_element_type=jnp.float32)
@@ -260,22 +264,22 @@
             out_ref[:, row, part] = turned.astype(jnp.bfloat16).reshape(grad_ref.shape[0], -1, points)
 
 
-def filter_call(flips, sent, spectrum, first_moment, second_moment):
+def filter_call(sent, spectrum, first_moment, second_moment):
     return pl.pallas_call(
         filter_kernel,
-        in_specs=[pl.BlockSpec(memory_space=pltpu.SMEM), whole, whole, whole, whole],
+        in_specs=[whole, whole, whole, whole],
         out_specs=whole,
         out_shape=jax.ShapeDtypeStruct(sent.shape, jnp.bfloat16),
         compiler_params=roomy,
         name="filter",
-    )(flips, sent, spectrum, first_moment, second_moment)
+    )(sent, spectrum, first_moment, second_moment)
 
 
 def update_kernel(
-    flip_ref, grad_ref, spec_ref, first_ref, second_ref, new_spec_ref, new_first_ref, new_second_ref
+    grad_ref, spec_ref, first_ref, second_ref, new_spec_ref, new_first_ref, new_second_ref
 ):
     points, width = spec_ref.shape[2:]
-    eye = square_eye(points, flip_ref[pl.program_id(0)] > 0)
+    eye = square_eye(points, is_mirrored(pl.program_id(0), pl.num_programs(0)))
     for part in range(2):
         sent = grad_ref[:, 0, part].reshape(width, points)
         grad = lax.dot_general(eye, sent, both_last, preferred_element_type=jnp.float32)
@@ -287,23 +291,20 @@
         new_second_ref[part, 0] = new_second
 
 
-def update_call(flips, sent, spectrum, first_moment, second_moment):
+def update_call(sent, spectrum, first_moment, second_moment):
     groups, local_outer, _, narrow, points = sent.shape
     channels = spectrum.shape[3]
-    state = pl.BlockSpec((2, 1, points, channels), lambda row, flags: (0, row, 0, 0))
-    wire = pl.BlockSpec((groups, 1, 2, narrow, points), lambda row, flags: (0, row, 0, 0, 0))
+    state = pl.BlockSpec((2, 1, points, channels), lambda row: (0, row, 0, 0))
+    wire = pl.BlockSpec((groups, 1, 2, narrow, points), lambda row: (0, row, 0, 0, 0))
     return pl.pallas_call(
         update_kernel,
-        grid_spec=pltpu.PrefetchScalarGridSpec(
-            num_scalar_prefetch=1,
-            grid=(local_outer,),
-            in_specs=[wire, state, state, state],
-            out_specs=[state, state, state],
-        ),
+        grid=(local_outer,),
+        in_specs=[wire, state, state, state],
+        out_specs=[state, state, state],
         out_shape=[jax.ShapeDtypeStruct(spectrum.shape, jnp.float32)] * 3,
         compiler_params=roomy,
         name="update",
-    )(flips, sent, spectrum, first_moment, second_moment)
+    )(sent, spectrum, first_moment, second_moment)
 
 
 def inverse_kernel(spectra_ref, filter_ref, twist_ref, matrix_ref, out_ref, mid_ref, *, chunk):
@@ -398,21 +399,26 @@
     return grad, jnp.stack([signal_re, signal_im], axis=1)
 
 
-def gradient_plain(flips, sent, shape):
+def mirrored_rows(local_outer):
+    rows = jnp.arange(local_outer, dtype=jnp.int32)
+    return is_mirrored(rows, local_outer)[None, :, None, None]
+
+
+def gradient_plain(sent, shape):
     arrived = sent.astype(jnp.float32).transpose(2, 1, 4, 0, 3).reshape(shape)
-    return jnp.where((flips > 0)[None, :, None, None], arrived[:, :, ::-1], arrived)
-
-
-def filter_plain(flips, sent, spectrum, first_moment, second_moment):
+    return jnp.where(mirrored_rows(shape[1]), arrived[:, :, ::-1], arrived)
+
+
+def filter_plain(sent, spectrum, first_moment, second_moment):
     groups, local_outer, _, narrow, points = sent.shape
-    grad = gradient_plain(flips, sent, spectrum.shape)
+    grad = gradient_plain(sent, spectrum.shape)
     new_spec, _, _ = moved(grad, spectrum, first_moment, second_moment)
-    out = jnp.where((flips > 0)[None, :, None, None], new_spec[:, :, ::-1], new_spec).astype(jnp.bfloat16)
+    out = jnp.where(mirrored_rows(local_outer), new_spec[:, :, ::-1], new_spec).astype(jnp.bfloat16)
     return out.reshape(2, local_outer, points, groups, narrow).transpose(3, 1, 0, 4, 2)
 
 
-def update_plain(flips, sent, spectrum, first_moment, second_moment):
-    return moved(gradient_plain(flips, sent, spectrum.shape), spectrum, first_moment, second_moment)
+def update_plain(sent, spectrum, first_moment, second_moment):
+    return moved(gradient_plain(sent, spectrum.shape), spectrum, first_moment, second_moment)
 
 
 def inverse_plain(spectra, filters, twist, matrices):
@@ -466,12 +472,10 @@
     grad = grad.reshape(seq_count, local_outer, 2, narrow, points)
     sent = lax.all_to_all(grad, "seq", split_axis=0, concat_axis=0, tiled=True)
 
-    residues = lax.axis_index("seq") * local_outer + jnp.arange(local_outer, dtype=jnp.int32)
-    flips = (residues > seq_count).astype(jnp.int32)
     states = (spectrum, first_moment, second_moment)
-    filters = (filter_call if tiled else filter_plain)(flips, sent, *states)
+    filters = (filter_call if tiled else filter_plain)(sent, *states)
     filters = lax.all_to_all(filters, "seq", split_axis=0, concat_axis=0, tiled=True)
-    new_spectrum, new_first, new_second = (update_call if tiled else update_plain)(flips, sent, *states)
+    new_spectrum, new_first, new_second = (update_call if tiled else update_plain)(sent, *states)
     filters = filters.reshape(outer, 2, narrow, points)
 
     rows = (inverse_call if tiled else inverse_plain)(spectra, filters, twist, back)

time: 134 us -> 127 us (0.948)
  blocking collectives: 65.7 us -> 91.4 us
  waiting for transfers between devices: 30.9 us -> 8.61 us
  local copies, waits for them, and re-layouts: 11.6 us -> 6.07 us
  starting transfers between devices: 8.1 us -> 4.24 us
    all_to_all x0 -> x1, blocking collectives: none -> 27.4 us  [per_device(): sent = lax.all_to_all(grad, 'seq', split_axis=0, concat_axis=0, tiled=True)]
    all_to_all x1 -> x0, waiting for transfers between devices: 22.8 us -> none  [per_device(): sent = lax.all_to_all(grad, 'seq', split_axis=0, concat_axis=0, tiled=True)]
    unnamed x28 -> x22, local copies, waits for them, and re-layouts: 11.6 us -> 6.07 us
    all_to_all x1 -> x0, starting transfers between devices: 3.66 us -> none  [per_device(): sent = lax.all_to_all(grad, 'seq', split_axis=0, concat_axis=0, tiled=True)]
    all_to_all x1, blocking collectives: 31.4 us -> 29.6 us  [per_device(): lax.all_to_all(filters, 'seq', split_axis=0, concat_axis=0, tiled=True)]
  transfers between devices with their start and end apart: 2 -> 1, of which waited for: 2 -> 1; matrix products, arithmetic and copies ran while one was open for 0% -> 0% of each run, Pallas kernels for 3% -> 3%
where the time goes in v3:
time: 127 us
  blocking collectives  91.4 us (72%)
  Pallas kernels  15.5 us (12%)
  waiting for transfers between devices  8.61 us (7%)
  local copies, waits for them, and re-layouts  6.07 us (5%)
  starting transfers between devices  4.24 us (3%)
    all_to_all x1, blocking collectives, per_device(): lax.all_to_all(packed, ('batch', 'seq'), split_axis=0, concat_axis=0, til...  34.3 us
    all_to_all x1, blocking collectives, per_device(): lax.all_to_all(filters, 'seq', split_axis=0, concat_axis=0, tiled=True)  29.6 us
    all_to_all x1, blocking collectives, per_device(): sent = lax.all_to_all(grad, 'seq', split_axis=0, concat_axis=0, tiled=True)  27.4 us
    all_to_all x1, waiting for transfers between devices, per_device(): lax.all_to_all(rows, ('batch', 'seq'), split_axis=0, concat_axis=0, tiled...  8.61 us
    unnamed x22, local copies, waits for them, and re-layouts  6.07 us
    pallas_call x1, Pallas kernels, forward_call(): pl.pallas_call(functools.partial(forward_kernel, scale=1.0 / (outer * poi...  4.69 us
    all_to_all x1, starting transfers between devices, per_device(): lax.all_to_all(rows, ('batch', 'seq'), split_axis=0, concat_axis=0, tiled...  4.24 us
    pallas_call x1, Pallas kernels, update_call(): pl.pallas_call(update_kernel, grid=(local_outer,), in_specs=[wire, state,...  4.07 us
  transfers between devices with their start and end apart: 1, of which 1 were waited for; matrix products, arithmetic and copies ran while one was open for 0% of the time, Pallas kernels for 3%

profile of v3, /device:TPU:0, one launch (start us, length us, event | category | flops | bytes accessed | tf_op | source)
XLA Modules:
  0.0 126.5 jit_solution(9166495540115008252)
XLA Ops:
  0.6 0.0 copy-start.8
  0.6 1.0 copy-done.8
  1.7 0.0 copy-start.9
  1.7 1.0 copy-done.9
  2.7 0.0 copy-start.10
  2.7 0.3 pack.1
  3.0 0.0 copy-start.3
  3.1 34.3 %all_to_all.20 = bf16[32,1,64,256]{3,2,1,0:T(8,128)(2,1)S(1)} all-to-all(bf16[32,1,64,256]{3,2,1,0:T(8,128)(2,1)S(1)} %bitcast.14), channel_id=1, replica_groups=mesh['seq'=16,'batch'=2] {'batch','seq'}, dimensions={0} | all-to-all | bytes 2097152 | tf_op jit(solution)/shard_map/all_to_all | solution.py:466
  37.4 0.0 copy-done.6
  37.4 0.0 copy-done.10
  37.4 0.0 copy-start
  37.4 0.0 copy-start.1
  37.4 4.7 %forward.1 = (bf16[32,2,32,256]{3,2,1,0:T(8,128)(2,1)S(1)}, f32[17,2,64,256]{3,2,1,0:T(8,128)S(1)}) custom-call(bf16[2,16,64,256]{3,2,1,0:T(8,128)(2,1)S(1)} %bitcast.13, f32[17,2,256]{2,1,0:T(2,128)S(1)} %copy-done.10, bf16[2,512,512]{2,1,0:T(8,128)(2,1)S(1)} %copy-done.6), custom_call_target="tpu_custom_call" | custom-call | tf_op jit(solution)/shard_map/forward/pallas_call | solution.py:229
  42.1 27.4 %all_to_all.21.grad_ref = bf16[16,2,2,32,256]{4,3,2,1,0:T(8,128)(2,1)S(1)} all-to-all(bf16[16,2,2,32,256]{4,3,2,1,0:T(8,128)(2,1)S(1)} %bitcast.17), channel_id=1, replica_groups=mesh['seq'=16,'batch'=2] {'seq'}, dimensions={0} | all-to-all | bytes 2097152 | tf_op jit(solution)/shard_map/all_to_all | solution.py:473
  69.5 0.0 copy-done.3
  69.5 0.0 copy-done
  69.5 0.0 copy-done.1
  69.5 1.9 %filter.1 = bf16[16,2,2,32,256]{4,3,2,1,0:T(8,128)(2,1)S(1)} custom-call(bf16[16,2,2,32,256]{4,3,2,1,0:T(8,128)(2,1)S(1)} %all_to_all.21.grad_ref, f32[2,2,256,512]{3,2,1,0:T(8,128)S(1)} %copy-done, f32[2,2,256,512]{3,2,1,0:T(8,128)S(1)} %copy-done.1, f32[2,2,256,512]{3,2,1,0:T(8,128)S(1)} %copy-done.3), custom_call_target="tpu_custom_call" | custom-call | tf_op jit(solution)/shard_map/filter/pallas_call | solution.py:268
  71.4 0.0 copy-start.7
  71.4 29.6 %all_to_all.22 = bf16[16,2,2,32,256]{4,3,2,1,0:T(8,128)(2,1)S(1)} all-to-all(bf16[16,2,2,32,256]{4,3,2,1,0:T(8,128)(2,1)S(1)} %filter.1), channel_id=1, replica_groups=mesh['seq'=16,'batch'=2] {'seq'}, dimensions={0} | all-to-all | bytes 2097152 | tf_op jit(solution)/shard_map/all_to_all | solution.py:477
  101.0 0.0 copy-done.7
  101.0 2.6 %inverse.1 = bf16[2,16,32,256]{3,2,1,0:T(8,128)(2,1)S(1)} custom-call(f32[17,2,64,256]{3,2,1,0:T(8,128)S(1)} %get-tuple-element.13.spectra_ref, bf16[32,2,32,256]{3,2,1,0:T(8,128)(2,1)S(1)} %bitcast.15, f32[17,2,256]{2,1,0:T(2,128)S(1)} %copy-done.10, bf16[2,512,512]{2,1,0:T(8,128)(2,1)S(1)} %copy-done.7), custom_call_target="tpu_custom_call" | custom-call | tf_op jit(solution)/shard_map/inverse/pallas_call | solution.py:361
  103.7 0.0 copy-start.5
  103.7 0.8 copy-done.5
  104.5 4.2 %all-to-all-start.3 = ((bf16[32,1,32,256]{3,2,1,0:T(8,128)(2,1)}), bf16[32,1,32,256]{3,2,1,0:T(8,128)(2,1)}, u32[]{:S(2)}, u32[]{:S(2)}) async-start(bf16[32,1,32,256]{3,2,1,0:T(8,128)(2,1)} %bitcast.16), calls=%async_computation.3 | async-start | bytes 1048576 | tf_op jit(solution)/shard_map/all_to_all | solution.py:484
  108.7 0.0 copy-start.2
  108.7 1.6 %copy-done.2 = f32[2,2,256,512]{3,2,1,0:T(8,128)S(1)} copy-done((f32[2,2,256,512]{3,2,1,0:T(8,128)S(1)}, f32[2,2,256,512]{3,2,1,0:T(8,128)}, u32[]{:S(2)}) %copy-start.2) | copy-done | bytes 2097176
  110.3 0.0 copy-start.4
  110.3 1.6 %copy-done.4 = f32[2,2,256,512]{3,2,1,0:T(8,128)S(1)} copy-done((f32[2,2,256,512]{3,2,1,0:T(8,128)S(1)}, f32[2,2,256,512]{3,2,1,0:T(8,128)}, u32[]{:S(2)}) %copy-start.4) | copy-done | bytes 2097176
  111.9 4.1 %update.1 = (f32[2,2,256,512]{3,2,1,0:T(8,128)}, f32[2,2,256,512]{3,2,1,0:T(8,128)}, f32[2,2,256,512]{3,2,1,0:T(8,128)}) custom-call(bf16[16,2,2,32,256]{4,3,2,1,0:T(8,128)(2,1)S(1)} %all_to_all.21.grad_ref, f32[2,2,256,512]{3,2,1,0:T(8,128)S(1)} %copy-done, f32[2,2,256,512]{3,2,1,0:T(8,128)S(1)} %copy-done.2, f32[2,2,256,512]{3,2,1,0:T(8,128)S(1)} %copy-done.4), custom_call_target="tpu_custom_call" | custom-call | tf_op jit(solution)/shard_map/update/pallas_call | solution.py:299
  116.0 8.6 %all-to-all-done.3 = bf16[32,1,32,256]{3,2,1,0:T(8,128)(2,1)} async-done(((bf16[32,1,32,256]{3,2,1,0:T(8,128)(2,1)}), bf16[32,1,32,256]{3,2,1,0:T(8,128)(2,1)}, u32[]{:S(2)}, u32[]{:S(2)}) %all-to-all-start.3) | async-done | bytes 524320 | tf_op jit(solution)/shard_map/all_to_all | solution.py:484
  124.6 1.9 %unpack.1 = bf16[256,1024]{1,0:T(8,128)(2,1)} custom-call(bf16[1024,256]{1,0:T(8,128)(2,1)} %bitcast.9.in_ref), custom_call_target="tpu_custom_call" | custom-call | tf_op jit(solution)/shard_map/unpack/pallas_call | solution.py:141
  (1 shorter events, 0.0 us)
Async XLA Ops:
  0.6 1.0 copy-start.8
  1.7 1.0 copy-start.9
  2.7 34.6 %copy-start.6 = (bf16[2,512,512]{2,1,0:T(8,128)(2,1)S(1)}, bf16[2,512,512]{2,1,0:T(8,128)(2,1)}, u32[]{:S(2)}) copy-start(bf16[2,512,512]{2,1,0:T(8,128)(2,1)} %constant.7.clone.matrix_ref) | copy-start | bytes 3145732
  2.7 34.7 %copy-start.10 = (f32[17,2,256]{2,1,0:T(2,128)S(1)}, f32[17,2,256]{2,1,0:T(2,128)}, u32[]{:S(2)}) copy-start(f32[17,2,256]{2,1,0:T(2,128)} %constant.6.clone.twist_ref) | copy-start | bytes 104452
  3.0 66.4 %copy-start.3 = (f32[2,2,256,512]{3,2,1,0:T(8,128)S(1)}, f32[2,2,256,512]{3,2,1,0:T(8,128)}, u32[]{:S(2)}) copy-start(f32[2,2,256,512]{3,2,1,0:T(8,128)} %second_ref.3) | copy-start | bytes 6291460
  37.4 32.1 %copy-start = (f32[2,2,256,512]{3,2,1,0:T(8,128)S(1)}, f32[2,2,256,512]{3,2,1,0:T(8,128)}, u32[]{:S(2)}) copy-start(f32[2,2,256,512]{3,2,1,0:T(8,128)} %spec_ref.3) | copy-start | bytes 6291460
  37.4 32.1 %copy-start.1 = (f32[2,2,256,512]{3,2,1,0:T(8,128)S(1)}, f32[2,2,256,512]{3,2,1,0:T(8,128)}, u32[]{:S(2)}) copy-start(f32[2,2,256,512]{3,2,1,0:T(8,128)} %first_ref.3) | copy-start | bytes 6291460
  71.4 29.7 %copy-start.7 = (bf16[2,512,512]{2,1,0:T(8,128)(2,1)S(1)}, bf16[2,512,512]{2,1,0:T(8,128)(2,1)}, u32[]{:S(2)}) copy-start(bf16[2,512,512]{2,1,0:T(8,128)(2,1)} %constant.8.clone.matrix_ref) | copy-start | bytes 3145732
  103.7 0.8 copy-start.5
  104.5 20.1 %all-to-all-start.3 = ((bf16[32,1,32,256]{3,2,1,0:T(8,128)(2,1)}), bf16[32,1,32,256]{3,2,1,0:T(8,128)(2,1)}, u32[]{:S(2)}, u32[]{:S(2)}) async-start(bf16[32,1,32,256]{3,2,1,0:T(8,128)(2,1)} %bitcast.16), calls=%async_computation.3 | async-start | bytes 1048576 | tf_op jit(solution)/shard_map/all_to_all | solution.py:484
  108.7 1.6 %copy-start.2 = (f32[2,2,256,512]{3,2,1,0:T(8,128)S(1)}, f32[2,2,256,512]{3,2,1,0:T(8,128)}, u32[]{:S(2)}) copy-start(f32[2,2,256,512]{3,2,1,0:T(8,128)} %first_ref.3) | copy-start | bytes 6291460
  110.3 1.6 %copy-start.4 = (f32[2,2,256,512]{3,2,1,0:T(8,128)S(1)}, f32[2,2,256,512]{3,2,1,0:T(8,128)}, u32[]{:S(2)}) copy-start(f32[2,2,256,512]{3,2,1,0:T(8,128)} %second_ref.3) | copy-start | bytes 6291460

commit v4 on v3

--- a/solution.py
+++ b/solution.py
@@ -137,12 +137,10 @@
 
 def unpack_call(rows):
     channels, points = rows.shape
-    width = math.gcd(channels, 512)
     return pl.pallas_call(
         unpack_kernel,
-        grid=(channels // width,),
-        in_specs=[pl.BlockSpec((width, points), lambda step: (step, 0))],
-        out_specs=pl.BlockSpec((points, width), lambda step: (0, step)),
+        in_specs=[whole],
+        out_specs=whole,
         out_shape=jax.ShapeDtypeStruct((points, channels), jnp.bfloat16),
         compiler_params=roomy,
         name="unpack",
@@ -161,11 +159,6 @@
     lax.fori_loop(0, count, step, 0)
     if (segments - 1) % chunk:
         emit(1 + count * chunk, (segments - 1) % chunk, True)
-
-
-def split_dot(values, matrices):
-    first = jnp.dot(values, matrices[0], preferred_element_type=jnp.float32)
-    return first + jnp.dot(values, matrices[1], preferred_element_type=jnp.float32)
 
 
 def forward_kernel(in_ref, twist_ref, matrix_ref, grad_ref, spectra_ref, mid_ref, *, scale, chunk):
@@ -201,7 +194,7 @@
 
     def emit(base, count, paired):
         values = mid_ref[pl.ds(base, count)].reshape(count * 2 * rows, 2 * points)
-        full = split_dot(values, matrix_ref).reshape(count, 2 * rows, 2 * points)
+        full = jnp.dot(values, matrix_ref[...], preferred_element_type=jnp.float32).reshape(count, 2 * rows, 2 * points)
         for extra in range(count):
             residue = base + extra
             signal_re, signal_im = full[extra, :rows, :points], full[extra, :rows, points:]
@@ -227,7 +220,7 @@
     outer = 2 * segments
     rows = sequences * narrow
     return pl.pallas_call(
-        functools.partial(forward_kernel, scale=1.0 / (outer * points), chunk=5),
+        functools.partial(forward_kernel, scale=1.0 / (outer * points), chunk=8),
         in_specs=[whole, whole, whole],
         out_specs=[whole, whole],
         out_shape=[
@@ -250,66 +243,51 @@
     return lax.axis_index("seq") * local_outer + row > lax.axis_size("seq")
 
 
-def filter_kernel(grad_ref, spec_ref, first_ref, second_ref, out_ref):
+def update_kernel(
+    grad_ref, spec_ref, first_ref, second_ref, new_spec_ref, new_first_ref, new_second_ref, out_ref
+):
     _, local_outer, points, width = spec_ref.shape
     for row in range(local_outer):
         eye = square_eye(points, is_mirrored(row, local_outer))
         for part in range(2):
             sent = grad_ref[:, row, part].reshape(width, points)
             grad = lax.dot_general(eye, sent, both_last, preferred_element_type=jnp.float32)
-            new_spec, _, _ = moved(grad, spec_ref[part, row], first_ref[part, row], second_ref[part, row])
+            new_spec, new_first, new_second = moved(
+                grad, spec_ref[part, row], first_ref[part, row], second_ref[part, row]
+            )
+            new_spec_ref[part, row] = new_spec
+            new_first_ref[part, row] = new_first
+            new_second_ref[part, row] = new_second
             turned = lax.dot_general(
                 new_spec.astype(jnp.bfloat16), eye, both_first, preferred_element_type=jnp.float32
             )
             out_ref[:, row, part] = turned.astype(jnp.bfloat16).reshape(grad_ref.shape[0], -1, points)
 
 
-def filter_call(sent, spectrum, first_moment, second_moment):
-    return pl.pallas_call(
-        filter_kernel,
-        in_specs=[whole, whole, whole, whole],
-        out_specs=whole,
-        out_shape=jax.ShapeDtypeStruct(sent.shape, jnp.bfloat16),
-        compiler_params=roomy,
-        name="filter",
-    )(sent, spectrum, first_moment, second_moment)
-
-
-def update_kernel(
-    grad_ref, spec_ref, first_ref, second_ref, new_spec_ref, new_first_ref, new_second_ref
-):
-    points, width = spec_ref.shape[2:]
-    eye = square_eye(points, is_mirrored(pl.program_id(0), pl.num_programs(0)))
-    for part in range(2):
-        sent = grad_ref[:, 0, part].reshape(width, points)
-        grad = lax.dot_general(eye, sent, both_last, preferred_element_type=jnp.float32)
-        new_spec, new_first, new_second = moved(
-            grad, spec_ref[part, 0], first_ref[part, 0], second_ref[part, 0]
-        )
-        new_spec_ref[part, 0] = new_spec
-        new_first_ref[part, 0] = new_first
-        new_second_ref[part, 0] = new_second
-
-
 def update_call(sent, spectrum, first_moment, second_moment):
-    groups, local_outer, _, narrow, points = sent.shape
-    channels = spectrum.shape[3]
-    state = pl.BlockSpec((2, 1, points, channels), lambda row: (0, row, 0, 0))
-    wire = pl.BlockSpec((groups, 1, 2, narrow, points), lambda row: (0, row, 0, 0, 0))
     return pl.pallas_call(
         update_kernel,
-        grid=(local_outer,),
-        in_specs=[wire, state, state, state],
-        out_specs=[state, state, state],
-        out_shape=[jax.ShapeDtypeStruct(spectrum.shape, jnp.float32)] * 3,
+        in_specs=[whole, whole, whole, whole],
+        out_specs=[whole, whole, whole, whole],
+        out_shape=[jax.ShapeDtypeStruct(spectrum.shape, jnp.float32)] * 3
+        + [jax.ShapeDtypeStruct(sent.shape, jnp.bfloat16)],
         compiler_params=roomy,
         name="update",
     )(sent, spectrum, first_moment, second_moment)
 
 
-def inverse_kernel(spectra_ref, filter_ref, twist_ref, matrix_ref, out_ref, mid_ref, *, chunk):
+def inverse_kernel(
+    spectra_ref, filter_ref, twist_ref, matrix_ref, *refs, chunk
+):
+    held, out_ref, final, mid_ref, leaving = refs[:3], refs[3], refs[4:7], refs[7], refs[8]
     sequences, segments, narrow, points = out_ref.shape
     rows = sequences * narrow
+    copies = [
+        pltpu.make_async_copy(source, target, leaving.at[index])
+        for index, (source, target) in enumerate(zip(held, final))
+    ]
+    for copy in copies:
+        copy.start()
 
     def mixed(residue, paired):
         filter_re = filter_ref[residue, 0].astype(jnp.float32)
@@ -325,7 +303,7 @@
 
     def emit(base, count, paired):
         values = jnp.concatenate([mixed(base + extra, paired) for extra in range(count)], axis=0)
-        full = split_dot(values, matrix_ref).reshape(count, rows, 2 * points)
+        full = jnp.dot(values, matrix_ref[...], preferred_element_type=jnp.float32).reshape(count, rows, 2 * points)
         for extra in range(count):
             residue = base + extra
             cos = twist_ref[residue, 0:1]
@@ -351,22 +329,29 @@
         return carry
 
     lax.fori_loop(0, sequences * tiles, tile_step, 0)
-
-
-def inverse_call(spectra, filters, twist, matrices):
+    for copy in copies:
+        copy.wait()
+
+
+def inverse_call(spectra, filters, twist, matrices, states):
     residues, _, rows, points = spectra.shape
     segments = residues - 1
     narrow = filters.shape[2]
     sequences = rows // narrow
-    return pl.pallas_call(
-        functools.partial(inverse_kernel, chunk=5),
-        in_specs=[whole, whole, whole, whole],
-        out_specs=whole,
-        out_shape=jax.ShapeDtypeStruct((sequences, segments, narrow, points), jnp.bfloat16),
-        scratch_shapes=[pltpu.VMEM((residues, 2, rows, points), jnp.float32)],
+    out, *states = pl.pallas_call(
+        functools.partial(inverse_kernel, chunk=8),
+        in_specs=[whole] * 7,
+        out_specs=[whole] + [pl.BlockSpec(memory_space=pl.ANY)] * 3,
+        out_shape=[jax.ShapeDtypeStruct((sequences, segments, narrow, points), jnp.bfloat16)]
+        + [jax.ShapeDtypeStruct(state.shape, state.dtype) for state in states],
+        scratch_shapes=[
+            pltpu.VMEM((residues, 2, rows, points), jnp.float32),
+            pltpu.SemaphoreType.DMA((3,)),
+        ],
         compiler_params=roomy,
         name="inverse",
-    )(spectra, filters, twist, matrices)
+    )(spectra, filters, twist, matrices, *states)
+    return out, states
 
 
 def pack_plain(signal, cotangent, narrow):
@@ -386,7 +371,7 @@
     im = jnp.stack([jnp.zeros_like(item[0]) if item[1] is None else item[1] for item in bins])
     cos, sin = twist[:, 0][:, None], twist[:, 1][:, None]
     mid = jnp.concatenate([re * cos + im * sin, im * cos - re * sin], axis=2).astype(jnp.bfloat16)
-    full = split_dot(mid, matrices)
+    full = jnp.dot(mid, matrices, preferred_element_type=jnp.float32)
     signal_re, signal_im = full[:, :rows, :points], full[:, :rows, points:]
     cotan_re, cotan_im = full[:, rows:, :points], full[:, rows:, points:]
     shape = (segments + 1, sequences, narrow, points)
@@ -409,19 +394,16 @@
     return jnp.where(mirrored_rows(shape[1]), arrived[:, :, ::-1], arrived)
 
 
-def filter_plain(sent, spectrum, first_moment, second_moment):
+def update_plain(sent, spectrum, first_moment, second_moment):
     groups, local_outer, _, narrow, points = sent.shape
     grad = gradient_plain(sent, spectrum.shape)
-    new_spec, _, _ = moved(grad, spectrum, first_moment, second_moment)
+    new_spec, new_first, new_second = moved(grad, spectrum, first_moment, second_moment)
     out = jnp.where(mirrored_rows(local_outer), new_spec[:, :, ::-1], new_spec).astype(jnp.bfloat16)
-    return out.reshape(2, local_outer, points, groups, narrow).transpose(3, 1, 0, 4, 2)
-
-
-def update_plain(sent, spectrum, first_moment, second_moment):
-    return moved(gradient_plain(sent, spectrum.shape), spectrum, first_moment, second_moment)
-
-
-def inverse_plain(spectra, filters, twist, matrices):
+    out = out.reshape(2, local_outer, points, groups, narrow).transpose(3, 1, 0, 4, 2)
+    return new_spec, new_first, new_second, out
+
+
+def inverse_plain(spectra, filters, twist, matrices, states):
     residues, _, rows, points = spectra.shape
     segments = residues - 1
     narrow = filters.shape[2]
@@ -434,19 +416,14 @@
     signal_re, signal_im = spectra[:, 0].reshape(shape), spectra[:, 1].reshape(shape)
     mixed_re = (signal_re * filter_re - signal_im * filter_im).reshape(residues, rows, points)
     mixed_im = (signal_re * filter_im + signal_im * filter_re).reshape(residues, rows, points)
-    full = split_dot(jnp.concatenate([mixed_re, mixed_im], axis=2).astype(jnp.bfloat16), matrices)
+    mixed = jnp.concatenate([mixed_re, mixed_im], axis=2).astype(jnp.bfloat16)
+    full = jnp.dot(mixed, matrices, preferred_element_type=jnp.float32)
     cos, sin = twist[:, 0][:, None], twist[:, 1][:, None]
     mid_re = full[..., :points] * cos - full[..., points:] * sin
     mid_im = full[..., :points] * sin + full[..., points:] * cos
     out = jnp.stack(real_segments([(mid_re[index], mid_im[index]) for index in range(residues)]))
     out = out.reshape(segments, sequences, narrow, points).transpose(1, 0, 2, 3)
-    return out.astype(jnp.bfloat16)
-
-
-def high_low(matrix):
-    high = matrix.astype(jnp.bfloat16)
-    low = (matrix - high.astype(np.float32)).astype(jnp.bfloat16)
-    return np.stack([high, low])
+    return out.astype(jnp.bfloat16), states
 
 
 def per_device(inputs, grad_out, spectrum, first_moment, second_moment):
@@ -459,7 +436,7 @@
     tiled = narrow % sub == 0 and points % lane == 0 and batch_rows == 1
     twist = jnp.asarray(twist_table(outer, points))
     ahead, back = point_matrices(points, 1.0 / (outer * points))
-    ahead, back = jnp.asarray(high_low(ahead)), jnp.asarray(high_low(back))
+    ahead, back = jnp.asarray(ahead, jnp.bfloat16), jnp.asarray(back, jnp.bfloat16)
 
     pack = pack_call if tiled else pack_plain
     packed = jnp.stack([pack(inputs[row], grad_out[row], narrow) for row in range(batch_rows)], axis=1)
@@ -472,13 +449,12 @@
     grad = grad.reshape(seq_count, local_outer, 2, narrow, points)
     sent = lax.all_to_all(grad, "seq", split_axis=0, concat_axis=0, tiled=True)
 
-    states = (spectrum, first_moment, second_moment)
-    filters = (filter_call if tiled else filter_plain)(sent, *states)
+    update = update_call if tiled else update_plain
+    *states, filters = update(sent, spectrum, first_moment, second_moment)
     filters = lax.all_to_all(filters, "seq", split_axis=0, concat_axis=0, tiled=True)
-    new_spectrum, new_first, new_second = (update_call if tiled else update_plain)(sent, *states)
     filters = filters.reshape(outer, 2, narrow, points)
 
-    rows = (inverse_call if tiled else inverse_plain)(spectra, filters, twist, back)
+    rows, states = (inverse_call if tiled else inverse_plain)(spectra, filters, twist, back, states)
     rows = rows.reshape(batch_count, batch_rows, seq_count, narrow, points).transpose(0, 2, 1, 3, 4)
     rows = rows.reshape(batch_count * seq_count, batch_rows, narrow, points)
     rows = lax.all_to_all(rows, ("batch", "seq"), split_axis=0, concat_axis=0, tiled=True)
@@ -486,7 +462,7 @@
         filtered = unpack_call(rows.reshape(channels, points))[None]
     else:
         filtered = rows.transpose(1, 3, 0, 2).reshape(batch_rows, points, channels)
-    return new_spectrum, new_first, new_second, filtered
+    return *states, filtered
 
 
 def solution(mesh):

time: 127 us -> 123 us (0.969)
  blocking collectives: 91.4 us -> 111 us
  waiting for transfers between devices: 8.61 us -> 0 us
  Pallas kernels: 15.5 us -> 9.04 us
  starting transfers between devices: 4.24 us -> 0 us
  local copies, waits for them, and re-layouts: 6.07 us -> 2.1 us
    all_to_all x0 -> x1, blocking collectives: none -> 19.8 us  [per_device(): lax.all_to_all(rows, ('batch', 'seq'), split_axis=0, concat_axis=0, tiled...]
    all_to_all x1 -> x0, waiting for transfers between devices: 8.61 us -> none  [per_device(): lax.all_to_all(rows, ('batch', 'seq'), split_axis=0, concat_axis=0, tiled...]
    pallas_call x4 -> x3, Pallas kernels: 10.5 us -> 5.69 us  [the longest x1 2.73 us: inverse_call(): pl.pallas_call(functools.partial(inverse_kernel, chunk=8), in_specs=[whol...]
    all_to_all x1 -> x0, starting transfers between devices: 4.24 us -> none  [per_device(): lax.all_to_all(rows, ('batch', 'seq'), split_axis=0, concat_axis=0, tiled...]
    unnamed x22 -> x16, local copies, waits for them, and re-layouts: 6.07 us -> 2.1 us
    pallas_call x1, Pallas kernels: 4.69 us -> 3.03 us  [forward_call(): pl.pallas_call(functools.partial(forward_kernel, scale=1.0 / (outer * poi...]
  transfers between devices with their start and end apart: 1 -> 0, of which waited for: 1 -> 0; matrix products, arithmetic and copies ran while one was open for 0% -> 0% of each run, Pallas kernels for 3% -> 0%
where the time goes in v4:
time: 123 us
  blocking collectives  111 us (90%)
  Pallas kernels  9.04 us (7%)
  local copies, waits for them, and re-layouts  2.1 us (2%)
    all_to_all x1, blocking collectives, per_device(): lax.all_to_all(packed, ('batch', 'seq'), split_axis=0, concat_axis=0, til...  34.3 us
    all_to_all x1, blocking collectives, per_device(): lax.all_to_all(filters, 'seq', split_axis=0, concat_axis=0, tiled=True)  29.6 us
    all_to_all x1, blocking collectives, per_device(): sent = lax.all_to_all(grad, 'seq', split_axis=0, concat_axis=0, tiled=True)  27.4 us
    all_to_all x1, blocking collectives, per_device(): lax.all_to_all(rows, ('batch', 'seq'), split_axis=0, concat_axis=0, tiled...  19.8 us
    pallas_call x1, Pallas kernels, forward_call(): pl.pallas_call(functools.partial(forward_kernel, scale=1.0 / (outer * poi...  3.03 us
    pallas_call x1, Pallas kernels, inverse_call(): pl.pallas_call(functools.partial(inverse_kernel, chunk=8), in_specs=[whol...  2.73 us

profile of v4, /device:TPU:0, one launch (start us, length us, event | category | flops | bytes accessed | tf_op | source)
XLA Modules:
  0.0 123.0 jit_solution(3392865972105241549)
XLA Ops:
  0.6 0.0 copy-start.5
  0.6 1.0 copy-done.5
  1.7 0.0 copy-start.6
  1.7 1.0 copy-done.6
  2.7 0.0 copy-start.4
  2.7 0.0 copy-start.7
  2.7 0.0 copy-start.2
  2.7 0.3 pack.1
  3.0 0.0 copy-start.1
  3.1 34.3 %all_to_all.20 = bf16[32,1,64,256]{3,2,1,0:T(8,128)(2,1)S(1)} all-to-all(bf16[32,1,64,256]{3,2,1,0:T(8,128)(2,1)S(1)} %bitcast.14), channel_id=1, replica_groups=mesh['seq'=16,'batch'=2] {'batch','seq'}, dimensions={0} | all-to-all | bytes 2097152 | tf_op jit(solution)/shard_map/all_to_all | solution.py:443
  37.4 0.0 copy-start
  37.4 0.0 copy-done.4
  37.4 0.0 copy-done.7
  37.4 3.0 %forward.1 = (bf16[32,2,32,256]{3,2,1,0:T(8,128)(2,1)S(1)}, f32[17,2,64,256]{3,2,1,0:T(8,128)S(1)}) custom-call(bf16[2,16,64,256]{3,2,1,0:T(8,128)(2,1)S(1)} %bitcast.13, f32[17,2,256]{2,1,0:T(2,128)S(1)} %copy-done.7, bf16[512,512]{1,0:T(8,128)(2,1)S(1)} %copy-done.4), custom_call_target="tpu_custom_call" | custom-call | tf_op jit(solution)/shard_map/forward/pallas_call | solution.py:222
  40.4 27.4 %all_to_all.21.grad_ref = bf16[16,2,2,32,256]{4,3,2,1,0:T(8,128)(2,1)S(1)} all-to-all(bf16[16,2,2,32,256]{4,3,2,1,0:T(8,128)(2,1)S(1)} %bitcast.17), channel_id=1, replica_groups=mesh['seq'=16,'batch'=2] {'seq'}, dimensions={0} | all-to-all | bytes 2097152 | tf_op jit(solution)/shard_map/all_to_all | solution.py:450
  67.8 0.0 copy-done.2
  67.8 0.0 copy-done.1
  67.8 0.0 copy-done
  67.8 2.0 %update.1 = (f32[2,2,256,512]{3,2,1,0:T(8,128)S(1)}, f32[2,2,256,512]{3,2,1,0:T(8,128)S(1)}, f32[2,2,256,512]{3,2,1,0:T(8,128)S(1)}, bf16[16,2,2,32,256]{4,3,2,1,0:T(8,128)(2,1)S(1)}) custom-call(bf16[16,2,2,32,256]{4,3,2,1,0:T(8,128)(2,1)S(1)} %all_to_all.21.grad_ref, f32[2,2,256,512]{3,2,1,0:T(8,128)S(1)} %copy-done, f32[2,2,256,512]{3,2,1,0:T(8,128)S(1)} %copy-done.1, ...), custom_call_target="tpu_custom_call" | custom-call | tf_op jit(solution)/shard_map/update/pallas_call | solution.py:268
  69.8 0.0 copy-start.3
  69.8 29.6 %all_to_all.22 = bf16[16,2,2,32,256]{4,3,2,1,0:T(8,128)(2,1)S(1)} all-to-all(bf16[16,2,2,32,256]{4,3,2,1,0:T(8,128)(2,1)S(1)} %get-tuple-element.16), channel_id=1, replica_groups=mesh['seq'=16,'batch'=2] {'seq'}, dimensions={0} | all-to-all | bytes 2097152 | tf_op jit(solution)/shard_map/all_to_all | solution.py:454
  99.5 0.0 copy-done.3
  99.5 2.7 %inverse.1 = (bf16[2,16,32,256]{3,2,1,0:T(8,128)(2,1)S(1)}, f32[2,2,256,512]{3,2,1,0:T(8,128)}, f32[2,2,256,512]{3,2,1,0:T(8,128)}, f32[2,2,256,512]{3,2,1,0:T(8,128)}) custom-call(f32[17,2,64,256]{3,2,1,0:T(8,128)S(1)} %get-tuple-element.14.spectra_ref, bf16[32,2,32,256]{3,2,1,0:T(8,128)(2,1)S(1)} %bitcast.15, f32[17,2,256]{2,1,0:T(2,128)S(1)} %copy-done.7, ...), custom_call_target="tpu_custom_call" | custom-call | tf_op jit(solution)/shard_map/inverse/pallas_call | solution.py:341
  102.2 19.8 %all_to_all.23 = bf16[32,1,32,256]{3,2,1,0:T(8,128)(2,1)S(1)} all-to-all(bf16[32,1,32,256]{3,2,1,0:T(8,128)(2,1)S(1)} %bitcast.18), channel_id=1, replica_groups=mesh['seq'=16,'batch'=2] {'batch','seq'}, dimensions={0} | all-to-all | bytes 1048576 | tf_op jit(solution)/shard_map/all_to_all | solution.py:460
  122.0 1.0 unpack.1
Async XLA Ops:
  0.6 1.0 copy-start.5
  1.7 1.0 copy-start.6
  2.7 34.7 %copy-start.4 = (bf16[512,512]{1,0:T(8,128)(2,1)S(1)}, bf16[512,512]{1,0:T(8,128)(2,1)}, u32[]{:S(2)}) copy-start(bf16[512,512]{1,0:T(8,128)(2,1)} %constant.7.clone.matrix_ref) | copy-start | bytes 1572868
  2.7 34.7 %copy-start.7 = (f32[17,2,256]{2,1,0:T(2,128)S(1)}, f32[17,2,256]{2,1,0:T(2,128)}, u32[]{:S(2)}) copy-start(f32[17,2,256]{2,1,0:T(2,128)} %constant.6.clone.twist_ref) | copy-start | bytes 104452
  2.7 65.1 %copy-start.2 = (f32[2,2,256,512]{3,2,1,0:T(8,128)S(1)}, f32[2,2,256,512]{3,2,1,0:T(8,128)}, u32[]{:S(2)}) copy-start(f32[2,2,256,512]{3,2,1,0:T(8,128)} %second_ref.1) | copy-start | bytes 6291460
  3.0 64.8 %copy-start.1 = (f32[2,2,256,512]{3,2,1,0:T(8,128)S(1)}, f32[2,2,256,512]{3,2,1,0:T(8,128)}, u32[]{:S(2)}) copy-start(f32[2,2,256,512]{3,2,1,0:T(8,128)} %first_ref.1) | copy-start | bytes 6291460
  37.4 30.5 %copy-start = (f32[2,2,256,512]{3,2,1,0:T(8,128)S(1)}, f32[2,2,256,512]{3,2,1,0:T(8,128)}, u32[]{:S(2)}) copy-start(f32[2,2,256,512]{3,2,1,0:T(8,128)} %spec_ref.1) | copy-start | bytes 6291460
  69.8 29.7 %copy-start.3 = (bf16[512,512]{1,0:T(8,128)(2,1)S(1)}, bf16[512,512]{1,0:T(8,128)(2,1)}, u32[]{:S(2)}) copy-start(bf16[512,512]{1,0:T(8,128)(2,1)} %constant.8.clone.matrix_ref) | copy-start | bytes 1572868

commit v5 on v4

--- a/solution.py
+++ b/solution.py
@@ -110,41 +110,78 @@
 roomy = pltpu.CompilerParams(vmem_limit_bytes=24 << 20)
 
 
-def pack_kernel(signal_ref, cotangent_ref, out_ref, *, narrow, width):
-    points, channels = signal_ref.shape
-    for part, source in enumerate((signal_ref, cotangent_ref)):
-        for left in range(0, channels, width):
-            turned = source[:, left : left + width].T.reshape(width // narrow, narrow, points)
-            first = left // narrow
-            out_ref[first : first + width // narrow, part * narrow : (part + 1) * narrow, :] = turned
+def pack_kernel(signal_hbm, cotangent_hbm, out_ref, held_ref, arrival, *, narrow):
+    blocks, points, width = held_ref.shape[1:]
+    each = width // narrow
+    copies = [
+        [
+            pltpu.make_async_copy(
+                source.at[:, block * width : (block + 1) * width],
+                held_ref.at[part, block],
+                arrival.at[part, block],
+            )
+            for part, source in enumerate((signal_hbm, cotangent_hbm))
+        ]
+        for block in range(blocks)
+    ]
+    for pair in copies:
+        for copy in pair:
+            copy.start()
+    for block, pair in enumerate(copies):
+        for part, copy in enumerate(pair):
+            copy.wait()
+            turned = held_ref[part, block].T.reshape(each, narrow, points)
+            out_ref[block * each : (block + 1) * each, part * narrow : (part + 1) * narrow, :] = turned
 
 
 def pack_call(signal, cotangent, narrow):
     points, channels = signal.shape
+    width = math.gcd(channels, 1024)
+    blocks = channels // width
+    signal = pltpu.with_memory_space_constraint(signal, pltpu.HBM)
+    cotangent = pltpu.with_memory_space_constraint(cotangent, pltpu.HBM)
     return pl.pallas_call(
-        functools.partial(pack_kernel, narrow=narrow, width=math.gcd(channels, 256)),
-        in_specs=[whole, whole],
+        functools.partial(pack_kernel, narrow=narrow),
+        in_specs=[pl.BlockSpec(memory_space=pltpu.HBM)] * 2,
         out_specs=whole,
         out_shape=jax.ShapeDtypeStruct((channels // narrow, 2 * narrow, points), jnp.bfloat16),
+        scratch_shapes=[
+            pltpu.VMEM((2, blocks, points, width), jnp.bfloat16),
+            pltpu.SemaphoreType.DMA((2, blocks)),
+        ],
         compiler_params=roomy,
         name="pack",
     )(signal, cotangent)
 
 
-def unpack_kernel(in_ref, out_ref):
+def departures(held, final, leaving):
+    return [
+        pltpu.make_async_copy(source, target, leaving.at[index])
+        for index, (source, target) in enumerate(zip(held, final))
+    ]
+
+
+def unpack_kernel(in_ref, held_ref, out_ref, final_ref, leaving):
+    copies = departures([held_ref], [final_ref], leaving)
+    copies[0].start()
     out_ref[...] = in_ref[...].T
-
-
-def unpack_call(rows):
+    copies[0].wait()
+
+
+def unpack_call(rows, state):
     channels, points = rows.shape
     return pl.pallas_call(
         unpack_kernel,
-        in_specs=[whole],
-        out_specs=whole,
-        out_shape=jax.ShapeDtypeStruct((points, channels), jnp.bfloat16),
+        in_specs=[whole, whole],
+        out_specs=[whole, pl.BlockSpec(memory_space=pl.ANY)],
+        out_shape=[
+            jax.ShapeDtypeStruct((points, channels), jnp.bfloat16),
+            jax.ShapeDtypeStruct(state.shape, state.dtype),
+        ],
+        scratch_shapes=[pltpu.SemaphoreType.DMA((1,))],
         compiler_params=roomy,
         name="unpack",
-    )(rows)
+    )(rows, state)
 
 
 def over_chunks(emit, segments, chunk):
@@ -276,18 +313,15 @@
     )(sent, spectrum, first_moment, second_moment)
 
 
-def inverse_kernel(
-    spectra_ref, filter_ref, twist_ref, matrix_ref, *refs, chunk
-):
-    held, out_ref, final, mid_ref, leaving = refs[:3], refs[3], refs[4:7], refs[7], refs[8]
+def inverse_kernel(spectra_ref, filter_ref, twist_ref, matrix_ref, *refs, chunk):
+    *moving, mid_ref, leaving = refs
+    count = len(moving) // 2
+    out_ref = moving[count]
+    copies = departures(moving[:count], moving[count + 1 :], leaving)
+    for copy in copies:
+        copy.start()
     sequences, segments, narrow, points = out_ref.shape
     rows = sequences * narrow
-    copies = [
-        pltpu.make_async_copy(source, target, leaving.at[index])
-        for index, (source, target) in enumerate(zip(held, final))
-    ]
-    for copy in copies:
-        copy.start()
 
     def mixed(residue, paired):
         filter_re = filter_ref[residue, 0].astype(jnp.float32)
@@ -340,13 +374,13 @@
     sequences = rows // narrow
     out, *states = pl.pallas_call(
         functools.partial(inverse_kernel, chunk=8),
-        in_specs=[whole] * 7,
-        out_specs=[whole] + [pl.BlockSpec(memory_space=pl.ANY)] * 3,
+        in_specs=[whole] * (4 + len(states)),
+        out_specs=[whole] + [pl.BlockSpec(memory_space=pl.ANY)] * len(states),
         out_shape=[jax.ShapeDtypeStruct((sequences, segments, narrow, points), jnp.bfloat16)]
         + [jax.ShapeDtypeStruct(state.shape, state.dtype) for state in states],
         scratch_shapes=[
             pltpu.VMEM((residues, 2, rows, points), jnp.float32),
-            pltpu.SemaphoreType.DMA((3,)),
+            pltpu.SemaphoreType.DMA((len(states),)),
         ],
         compiler_params=roomy,
         name="inverse",
@@ -450,19 +484,21 @@
     sent = lax.all_to_all(grad, "seq", split_axis=0, concat_axis=0, tiled=True)
 
     update = update_call if tiled else update_plain
-    *states, filters = update(sent, spectrum, first_moment, second_moment)
+    new_spectrum, new_first, new_second, filters = update(sent, spectrum, first_moment, second_moment)
     filters = lax.all_to_all(filters, "seq", split_axis=0, concat_axis=0, tiled=True)
     filters = filters.reshape(outer, 2, narrow, points)
 
-    rows, states = (inverse_call if tiled else inverse_plain)(spectra, filters, twist, back, states)
+    early = [new_spectrum, new_first]
+    rows, early = (inverse_call if tiled else inverse_plain)(spectra, filters, twist, back, early)
     rows = rows.reshape(batch_count, batch_rows, seq_count, narrow, points).transpose(0, 2, 1, 3, 4)
     rows = rows.reshape(batch_count * seq_count, batch_rows, narrow, points)
     rows = lax.all_to_all(rows, ("batch", "seq"), split_axis=0, concat_axis=0, tiled=True)
     if tiled:
-        filtered = unpack_call(rows.reshape(channels, points))[None]
+        filtered, new_second = unpack_call(rows.reshape(channels, points), new_second)
+        filtered = filtered[None]
     else:
         filtered = rows.transpose(1, 3, 0, 2).reshape(batch_rows, points, channels)
-    return *states, filtered
+    return *early, new_second, filtered
 
 
 def solution(mesh):

time: 123 us -> 123 us (level)
  local copies, waits for them, and re-layouts: 2.1 us -> 0.03 us
  Pallas kernels: 9.04 us -> 10.8 us
    pallas_call x2, Pallas kernels: 1.31 us -> 3.76 us  [the longest x1 2.16 us: unpack_call(): pl.pallas_call(unpack_kernel, in_specs=[whole, whole], out_specs=[whole,...]
    unnamed x16 -> x12, local copies, waits for them, and re-layouts: 2.1 us -> 0.03 us
where the time goes in v5:
time: 123 us
  blocking collectives  111 us (90%)
  Pallas kernels  10.8 us (9%)
    all_to_all x1, blocking collectives, per_device(): lax.all_to_all(packed, ('batch', 'seq'), split_axis=0, concat_axis=0, til...  34.3 us
    all_to_all x1, blocking collectives, per_device(): lax.all_to_all(filters, 'seq', split_axis=0, concat_axis=0, tiled=True)  29.6 us
    all_to_all x1, blocking collectives, per_device(): sent = lax.all_to_all(grad, 'seq', split_axis=0, concat_axis=0, tiled=True)  27.4 us
    all_to_all x1, blocking collectives, per_device(): lax.all_to_all(rows, ('batch', 'seq'), split_axis=0, concat_axis=0, tiled...  19.8 us
    pallas_call x1, Pallas kernels, forward_call(): pl.pallas_call(functools.partial(forward_kernel, scale=1.0 / (outer * poi...  3.03 us

profile of v5, /device:TPU:0, one launch (start us, length us, event | category | flops | bytes accessed | tf_op | source)
XLA Modules:
  0.0 122.7 jit_solution(2330508536734662054)
XLA Ops:
  0.6 0.0 copy-start.4
  0.6 0.0 copy-start.5
  0.7 0.0 copy-start.2
  0.7 1.6 %pack.1 = bf16[32,64,256]{2,1,0:T(8,128)(2,1)S(1)} custom-call(bf16[256,1024]{1,0:T(8,128)(2,1)} %bitcast.19, bf16[256,1024]{1,0:T(8,128)(2,1)} %bitcast.20), custom_call_target="tpu_custom_call" | custom-call | tf_op jit(solution)/shard_map/pack/pallas_call | solution.py:143
  2.3 0.0 copy-start.1
  2.3 34.3 %all_to_all.20 = bf16[32,1,64,256]{3,2,1,0:T(8,128)(2,1)S(1)} all-to-all(bf16[32,1,64,256]{3,2,1,0:T(8,128)(2,1)S(1)} %bitcast.15), channel_id=1, replica_groups=mesh['seq'=16,'batch'=2] {'batch','seq'}, dimensions={0} | all-to-all | bytes 2097152 | tf_op jit(solution)/shard_map/all_to_all | solution.py:477
  36.6 0.0 copy-start
  36.6 0.0 copy-done.4
  36.6 0.0 copy-done.5
  36.6 3.0 %forward.1 = (bf16[32,2,32,256]{3,2,1,0:T(8,128)(2,1)S(1)}, f32[17,2,64,256]{3,2,1,0:T(8,128)S(1)}) custom-call(bf16[2,16,64,256]{3,2,1,0:T(8,128)(2,1)S(1)} %bitcast.14, f32[17,2,256]{2,1,0:T(2,128)S(1)} %copy-done.5, bf16[512,512]{1,0:T(8,128)(2,1)S(1)} %copy-done.4), custom_call_target="tpu_custom_call" | custom-call | tf_op jit(solution)/shard_map/forward/pallas_call | solution.py:259
  39.6 27.4 %all_to_all.21.grad_ref = bf16[16,2,2,32,256]{4,3,2,1,0:T(8,128)(2,1)S(1)} all-to-all(bf16[16,2,2,32,256]{4,3,2,1,0:T(8,128)(2,1)S(1)} %bitcast.17), channel_id=1, replica_groups=mesh['seq'=16,'batch'=2] {'seq'}, dimensions={0} | all-to-all | bytes 2097152 | tf_op jit(solution)/shard_map/all_to_all | solution.py:484
  67.0 0.0 copy-done.2
  67.0 0.0 copy-done.1
  67.0 0.0 copy-done
  67.0 2.0 %update.1 = (f32[2,2,256,512]{3,2,1,0:T(8,128)S(1)}, f32[2,2,256,512]{3,2,1,0:T(8,128)S(1)}, f32[2,2,256,512]{3,2,1,0:T(8,128)S(1)}, bf16[16,2,2,32,256]{4,3,2,1,0:T(8,128)(2,1)S(1)}) custom-call(bf16[16,2,2,32,256]{4,3,2,1,0:T(8,128)(2,1)S(1)} %all_to_all.21.grad_ref, f32[2,2,256,512]{3,2,1,0:T(8,128)S(1)} %copy-done, f32[2,2,256,512]{3,2,1,0:T(8,128)S(1)} %copy-done.1, ...), custom_call_target="tpu_custom_call" | custom-call | tf_op jit(solution)/shard_map/update/pallas_call | solution.py:305
  69.0 0.0 copy-start.3
  69.0 29.6 %all_to_all.22 = bf16[16,2,2,32,256]{4,3,2,1,0:T(8,128)(2,1)S(1)} all-to-all(bf16[16,2,2,32,256]{4,3,2,1,0:T(8,128)(2,1)S(1)} %get-tuple-element.17), channel_id=1, replica_groups=mesh['seq'=16,'batch'=2] {'seq'}, dimensions={0} | all-to-all | bytes 2097152 | tf_op jit(solution)/shard_map/all_to_all | solution.py:488
  98.7 0.0 copy-done.3
  98.7 2.0 %inverse.1 = (bf16[2,16,32,256]{3,2,1,0:T(8,128)(2,1)S(1)}, f32[2,2,256,512]{3,2,1,0:T(8,128)}, f32[2,2,256,512]{3,2,1,0:T(8,128)}) custom-call(f32[17,2,64,256]{3,2,1,0:T(8,128)S(1)} %get-tuple-element.15.spectra_ref, bf16[32,2,32,256]{3,2,1,0:T(8,128)(2,1)S(1)} %bitcast.13, f32[17,2,256]{2,1,0:T(2,128)S(1)} %copy-done.5, bf16[512,512]{1,0:T(8,128)(2,1)S(1)} %copy-done.3, ...), custom_call_target="tpu_custom_call" | custom-call | tf_op jit(solution)/shard_map/inverse/pallas_call | solution.py:375
  100.7 19.8 %all_to_all.23 = bf16[32,1,32,256]{3,2,1,0:T(8,128)(2,1)S(1)} all-to-all(bf16[32,1,32,256]{3,2,1,0:T(8,128)(2,1)S(1)} %bitcast.18), channel_id=1, replica_groups=mesh['seq'=16,'batch'=2] {'batch','seq'}, dimensions={0} | all-to-all | bytes 1048576 | tf_op jit(solution)/shard_map/all_to_all | solution.py:495
  120.5 2.2 %unpack.1 = (bf16[256,1024]{1,0:T(8,128)(2,1)}, f32[2,2,256,512]{3,2,1,0:T(8,128)}) custom-call(bf16[1024,256]{1,0:T(8,128)(2,1)S(1)} %bitcast.16, f32[2,2,256,512]{3,2,1,0:T(8,128)S(1)} %get-tuple-element.23.held_ref), custom_call_target="tpu_custom_call" | custom-call | tf_op jit(solution)/shard_map/unpack/pallas_call | solution.py:173
Async XLA Ops:
  0.6 36.0 %copy-start.4 = (bf16[512,512]{1,0:T(8,128)(2,1)S(1)}, bf16[512,512]{1,0:T(8,128)(2,1)}, u32[]{:S(2)}) copy-start(bf16[512,512]{1,0:T(8,128)(2,1)} %constant.7.clone.matrix_ref) | copy-start | bytes 1572868
  0.6 35.9 %copy-start.5 = (f32[17,2,256]{2,1,0:T(2,128)S(1)}, f32[17,2,256]{2,1,0:T(2,128)}, u32[]{:S(2)}) copy-start(f32[17,2,256]{2,1,0:T(2,128)} %constant.6.clone.twist_ref) | copy-start | bytes 104452
  0.7 66.4 %copy-start.2 = (f32[2,2,256,512]{3,2,1,0:T(8,128)S(1)}, f32[2,2,256,512]{3,2,1,0:T(8,128)}, u32[]{:S(2)}) copy-start(f32[2,2,256,512]{3,2,1,0:T(8,128)} %second_ref.1) | copy-start | bytes 6291460
  2.3 64.8 %copy-start.1 = (f32[2,2,256,512]{3,2,1,0:T(8,128)S(1)}, f32[2,2,256,512]{3,2,1,0:T(8,128)}, u32[]{:S(2)}) copy-start(f32[2,2,256,512]{3,2,1,0:T(8,128)} %first_ref.1) | copy-start | bytes 6291460
  36.6 30.5 %copy-start = (f32[2,2,256,512]{3,2,1,0:T(8,128)S(1)}, f32[2,2,256,512]{3,2,1,0:T(8,128)}, u32[]{:S(2)}) copy-start(f32[2,2,256,512]{3,2,1,0:T(8,128)} %spec_ref.1) | copy-start | bytes 6291460
  69.0 29.7 %copy-start.3 = (bf16[512,512]{1,0:T(8,128)(2,1)S(1)}, bf16[512,512]{1,0:T(8,128)(2,1)}, u32[]{:S(2)}) copy-start(bf16[512,512]{1,0:T(8,128)(2,1)} %constant.8.clone.matrix_ref) | copy-start | bytes 1572868

commit v6 on v4

--- a/solution.py
+++ b/solution.py
@@ -107,32 +107,61 @@
 
 
 whole = pl.BlockSpec(memory_space=pltpu.VMEM)
+outside = pl.BlockSpec(memory_space=pl.ANY)
 roomy = pltpu.CompilerParams(vmem_limit_bytes=24 << 20)
 
 
-def pack_kernel(signal_ref, cotangent_ref, out_ref, *, narrow, width):
-    points, channels = signal_ref.shape
-    for part, source in enumerate((signal_ref, cotangent_ref)):
-        for left in range(0, channels, width):
-            turned = source[:, left : left + width].T.reshape(width // narrow, narrow, points)
-            first = left // narrow
-            out_ref[first : first + width // narrow, part * narrow : (part + 1) * narrow, :] = turned
+def copies_of(pairs, marks, pieces):
+    made = []
+    for index, (source, target) in enumerate(pairs):
+        length = source.shape[0] // pieces
+        for piece in range(pieces):
+            here = slice(piece * length, (piece + 1) * length)
+            made.append(pltpu.make_async_copy(source.at[here], target.at[here], marks.at[index, piece]))
+    return made
+
+
+def pack_kernel(signal_hbm, cotangent_hbm, out_ref, held_ref, arrival, *, narrow):
+    points, channels = signal_hbm.shape
+    sources = (signal_hbm, cotangent_hbm)
+    copies = copies_of([(source, held_ref.at[part]) for part, source in enumerate(sources)], arrival, 1)
+    for copy in copies:
+        copy.start()
+    for part in range(2):
+        for copy in copies[part : part + 1]:
+            copy.wait()
+        turned = held_ref[part].T.reshape(channels // narrow, narrow, points)
+        out_ref[:, part * narrow : (part + 1) * narrow, :] = turned
 
 
 def pack_call(signal, cotangent, narrow):
     points, channels = signal.shape
+    signal = pltpu.with_memory_space_constraint(signal, pltpu.HBM)
+    cotangent = pltpu.with_memory_space_constraint(cotangent, pltpu.HBM)
     return pl.pallas_call(
-        functools.partial(pack_kernel, narrow=narrow, width=math.gcd(channels, 256)),
-        in_specs=[whole, whole],
+        functools.partial(pack_kernel, narrow=narrow),
+        in_specs=[pl.BlockSpec(memory_space=pltpu.HBM)] * 2,
         out_specs=whole,
         out_shape=jax.ShapeDtypeStruct((channels // narrow, 2 * narrow, points), jnp.bfloat16),
+        scratch_shapes=[
+            pltpu.VMEM((2, points, channels), jnp.bfloat16),
+            pltpu.SemaphoreType.DMA((2, 1)),
+        ],
         compiler_params=roomy,
         name="pack",
     )(signal, cotangent)
 
 
-def unpack_kernel(in_ref, out_ref):
-    out_ref[...] = in_ref[...].T
+def unpack_kernel(in_ref, out_hbm, held_ref, leaving):
+    channels, points = in_ref.shape
+    length = points // 2
+    copies = copies_of([(held_ref, out_hbm)], leaving, 2)
+    for piece, copy in enumerate(copies):
+        here = slice(piece * length, (piece + 1) * length)
+        held_ref[here, :] = in_ref[:, here].T
+        copy.start()
+    for copy in copies:
+        copy.wait()
 
 
 def unpack_call(rows):
@@ -140,8 +169,9 @@
     return pl.pallas_call(
         unpack_kernel,
         in_specs=[whole],
-        out_specs=whole,
+        out_specs=pl.BlockSpec(memory_space=pl.ANY),
         out_shape=jax.ShapeDtypeStruct((points, channels), jnp.bfloat16),
+        scratch_shapes=[pltpu.VMEM((points, channels), jnp.bfloat16), pltpu.SemaphoreType.DMA((1, 2))],
         compiler_params=roomy,
         name="unpack",
     )(rows)
@@ -243,51 +273,68 @@
     return lax.axis_index("seq") * local_outer + row > lax.axis_size("seq")
 
 
-def update_kernel(
-    grad_ref, spec_ref, first_ref, second_ref, new_spec_ref, new_first_ref, new_second_ref, out_ref
-):
+def update_kernel(grad_ref, spec_ref, first_ref, second_ref, *refs):
+    final, held, (out_ref, *ready, leaving) = refs[:3], refs[3:6], refs[6:]
     _, local_outer, points, width = spec_ref.shape
+    early = ready[0].shape[1]
+    copies = []
     for row in range(local_outer):
         eye = square_eye(points, is_mirrored(row, local_outer))
         for part in range(2):
             sent = grad_ref[:, row, part].reshape(width, points)
             grad = lax.dot_general(eye, sent, both_last, preferred_element_type=jnp.float32)
-            new_spec, new_first, new_second = moved(
-                grad, spec_ref[part, row], first_ref[part, row], second_ref[part, row]
-            )
-            new_spec_ref[part, row] = new_spec
-            new_first_ref[part, row] = new_first
-            new_second_ref[part, row] = new_second
+            made = moved(grad, spec_ref[part, row], first_ref[part, row], second_ref[part, row])
+            for index in range(3):
+                if row < early:
+                    ready[index][part, row] = made[index]
+                    copies.append(
+                        pltpu.make_async_copy(
+                            ready[index].at[part, row], final[index].at[part, row], leaving.at[index, part, row]
+                        )
+                    )
+                    copies[-1].start()
+                else:
+                    held[index][part, row - early] = made[index]
             turned = lax.dot_general(
-                new_spec.astype(jnp.bfloat16), eye, both_first, preferred_element_type=jnp.float32
+                made[0].astype(jnp.bfloat16), eye, both_first, preferred_element_type=jnp.float32
             )
             out_ref[:, row, part] = turned.astype(jnp.bfloat16).reshape(grad_ref.shape[0], -1, points)
+    for copy in copies:
+        copy.wait()
 
 
 def update_call(sent, spectrum, first_moment, second_moment):
-    return pl.pallas_call(
+    parts, local_outer, points, channels = spectrum.shape
+    early = (local_outer + 1) // 2
+    late = (parts, local_outer - early, points, channels)
+    made = pl.pallas_call(
         update_kernel,
         in_specs=[whole, whole, whole, whole],
-        out_specs=[whole, whole, whole, whole],
+        out_specs=[outside] * 3 + [whole] * 4,
         out_shape=[jax.ShapeDtypeStruct(spectrum.shape, jnp.float32)] * 3
+        + [jax.ShapeDtypeStruct(late, jnp.float32)] * 3
         + [jax.ShapeDtypeStruct(sent.shape, jnp.bfloat16)],
+        scratch_shapes=[pltpu.VMEM((parts, early, points, channels), jnp.float32)] * 3
+        + [pltpu.SemaphoreType.DMA((3, parts, early))],
         compiler_params=roomy,
         name="update",
     )(sent, spectrum, first_moment, second_moment)
-
-
-def inverse_kernel(
-    spectra_ref, filter_ref, twist_ref, matrix_ref, *refs, chunk
-):
-    held, out_ref, final, mid_ref, leaving = refs[:3], refs[3], refs[4:7], refs[7], refs[8]
+    return (made[:3], made[3:6]), made[6]
+
+
+def inverse_kernel(spectra_ref, filter_ref, twist_ref, matrix_ref, *refs, chunk):
+    held, out_ref, final, mid_ref, leaving = refs[:3], refs[6], refs[7:10], refs[10], refs[11]
+    early = final[0].shape[1] - held[0].shape[1]
+    pairs = [
+        (source.at[part], target.at[part, early:])
+        for source, target in zip(held, final)
+        for part in range(source.shape[0])
+    ]
+    copies = copies_of(pairs, leaving, 1)
+    for copy in copies:
+        copy.start()
     sequences, segments, narrow, points = out_ref.shape
     rows = sequences * narrow
-    copies = [
-        pltpu.make_async_copy(source, target, leaving.at[index])
-        for index, (source, target) in enumerate(zip(held, final))
-    ]
-    for copy in copies:
-        copy.start()
 
     def mixed(residue, paired):
         filter_re = filter_ref[residue, 0].astype(jnp.float32)
@@ -334,24 +381,26 @@
 
 
 def inverse_call(spectra, filters, twist, matrices, states):
+    final, held = states
     residues, _, rows, points = spectra.shape
     segments = residues - 1
     narrow = filters.shape[2]
     sequences = rows // narrow
-    out, *states = pl.pallas_call(
+    out, *final = pl.pallas_call(
         functools.partial(inverse_kernel, chunk=8),
-        in_specs=[whole] * 7,
-        out_specs=[whole] + [pl.BlockSpec(memory_space=pl.ANY)] * 3,
+        in_specs=[whole] * 7 + [outside] * 3,
+        out_specs=[whole] + [outside] * 3,
         out_shape=[jax.ShapeDtypeStruct((sequences, segments, narrow, points), jnp.bfloat16)]
-        + [jax.ShapeDtypeStruct(state.shape, state.dtype) for state in states],
+        + [jax.ShapeDtypeStruct(state.shape, state.dtype) for state in final],
+        input_output_aliases={7: 1, 8: 2, 9: 3},
         scratch_shapes=[
             pltpu.VMEM((residues, 2, rows, points), jnp.float32),
-            pltpu.SemaphoreType.DMA((3,)),
+            pltpu.SemaphoreType.DMA((6, 1)),
         ],
         compiler_params=roomy,
         name="inverse",
-    )(spectra, filters, twist, matrices, *states)
-    return out, states
+    )(spectra, filters, twist, matrices, *held, *final)
+    return out, final
 
 
 def pack_plain(signal, cotangent, narrow):
@@ -400,7 +449,7 @@
     new_spec, new_first, new_second = moved(grad, spectrum, first_moment, second_moment)
     out = jnp.where(mirrored_rows(local_outer), new_spec[:, :, ::-1], new_spec).astype(jnp.bfloat16)
     out = out.reshape(2, local_outer, points, groups, narrow).transpose(3, 1, 0, 4, 2)
-    return new_spec, new_first, new_second, out
+    return (new_spec, new_first, new_second), out
 
 
 def inverse_plain(spectra, filters, twist, matrices, states):
@@ -450,7 +499,7 @@
     sent = lax.all_to_all(grad, "seq", split_axis=0, concat_axis=0, tiled=True)
 
     update = update_call if tiled else update_plain
-    *states, filters = update(sent, spectrum, first_moment, second_moment)
+    states, filters = update(sent, spectrum, first_moment, second_moment)
     filters = lax.all_to_all(filters, "seq", split_axis=0, concat_axis=0, tiled=True)
     filters = filters.reshape(outer, 2, narrow, points)
 

time: 123 us -> 122 us (level)
  local copies, waits for them, and re-layouts: 2.1 us -> 0.03 us
    unnamed x16 -> x12, local copies, waits for them, and re-layouts: 2.1 us -> 0.03 us
where the time goes in v6:
time: 122 us
  blocking collectives  111 us (91%)
  Pallas kernels  9.98 us (8%)
    all_to_all x1, blocking collectives, per_device(): lax.all_to_all(packed, ('batch', 'seq'), split_axis=0, concat_axis=0, til...  34.3 us
    all_to_all x1, blocking collectives, per_device(): lax.all_to_all(filters, 'seq', split_axis=0, concat_axis=0, tiled=True)  29.6 us
    all_to_all x1, blocking collectives, per_device(): sent = lax.all_to_all(grad, 'seq', split_axis=0, concat_axis=0, tiled=True)  27.4 us
    all_to_all x1, blocking collectives, per_device(): lax.all_to_all(rows, ('batch', 'seq'), split_axis=0, concat_axis=0, tiled...  19.8 us
    pallas_call x1, Pallas kernels, forward_call(): pl.pallas_call(functools.partial(forward_kernel, scale=1.0 / (outer * poi...  3.03 us
    pallas_call x1, Pallas kernels, update_call(): pl.pallas_call(update_kernel, in_specs=[whole, whole, whole, whole], out_...  2.72 us

profile of v6, /device:TPU:0, one launch (start us, length us, event | category | flops | bytes accessed | tf_op | source)
XLA Modules:
  0.0 121.9 jit_solution(11089932777887970701)
XLA Ops:
  0.6 0.0 copy-start.4
  0.6 0.0 copy-start.5
  0.7 0.0 copy-start.2
  0.7 1.6 %pack.1 = bf16[32,64,256]{2,1,0:T(8,128)(2,1)S(1)} custom-call(bf16[256,1024]{1,0:T(8,128)(2,1)} %bitcast.20, bf16[256,1024]{1,0:T(8,128)(2,1)} %bitcast.21), custom_call_target="tpu_custom_call" | custom-call | tf_op jit(solution)/shard_map/pack/pallas_call | solution.py:141
  2.3 0.0 copy-start.1
  2.3 34.3 %all_to_all.20 = bf16[32,1,64,256]{3,2,1,0:T(8,128)(2,1)S(1)} all-to-all(bf16[32,1,64,256]{3,2,1,0:T(8,128)(2,1)S(1)} %bitcast.14), channel_id=1, replica_groups=mesh['seq'=16,'batch'=2] {'batch','seq'}, dimensions={0} | all-to-all | bytes 2097152 | tf_op jit(solution)/shard_map/all_to_all | solution.py:492
  36.6 0.0 copy-start
  36.6 0.0 copy-done.4
  36.6 0.0 copy-done.5
  36.6 3.0 %forward.1 = (bf16[32,2,32,256]{3,2,1,0:T(8,128)(2,1)S(1)}, f32[17,2,64,256]{3,2,1,0:T(8,128)S(1)}) custom-call(bf16[2,16,64,256]{3,2,1,0:T(8,128)(2,1)S(1)} %bitcast.13, f32[17,2,256]{2,1,0:T(2,128)S(1)} %copy-done.5, bf16[512,512]{1,0:T(8,128)(2,1)S(1)} %copy-done.4), custom_call_target="tpu_custom_call" | custom-call | tf_op jit(solution)/shard_map/forward/pallas_call | solution.py:252
  39.6 27.4 %all_to_all.21.grad_ref = bf16[16,2,2,32,256]{4,3,2,1,0:T(8,128)(2,1)S(1)} all-to-all(bf16[16,2,2,32,256]{4,3,2,1,0:T(8,128)(2,1)S(1)} %bitcast.17), channel_id=1, replica_groups=mesh['seq'=16,'batch'=2] {'seq'}, dimensions={0} | all-to-all | bytes 2097152 | tf_op jit(solution)/shard_map/all_to_all | solution.py:499
  67.0 0.0 copy-done.2
  67.0 0.0 copy-done.1
  67.0 0.0 copy-done
  67.0 2.7 %update.1 = (f32[2,2,256,512]{3,2,1,0:T(8,128)}, f32[2,2,256,512]{3,2,1,0:T(8,128)}, f32[2,2,256,512]{3,2,1,0:T(8,128)}, f32[2,1,256,512]{3,2,1,0:T(8,128)S(1)},...) custom-call(bf16[16,2,2,32,256]{4,3,2,1,0:T(8,128)(2,1)S(1)} %all_to_all.21, ...), custom_call_target="tpu_custom_call" | custom-call | tf_op jit(solution)/shard_map/update/pallas_call | solution.py:310
  69.8 0.0 copy-start.3
  69.8 29.6 %all_to_all.22 = bf16[16,2,2,32,256]{4,3,2,1,0:T(8,128)(2,1)S(1)} all-to-all(bf16[16,2,2,32,256]{4,3,2,1,0:T(8,128)(2,1)S(1)} %get-tuple-element.19), channel_id=1, replica_groups=mesh['seq'=16,'batch'=2] {'seq'}, dimensions={0} | all-to-all | bytes 2097152 | tf_op jit(solution)/shard_map/all_to_all | solution.py:503
  99.4 0.0 copy-done.3
  99.4 1.7 %inverse.1 = (bf16[2,16,32,256]{3,2,1,0:T(8,128)(2,1)S(1)}, f32[2,2,256,512]{3,2,1,0:T(8,128)}, f32[2,2,256,512]{3,2,1,0:T(8,128)}, f32[2,2,256,512]{3,2,1,0:T(8,128)}) custom-call(f32[17,2,64,256]{3,2,1,0:T(8,128)S(1)} %get-tuple-element.17.spectra_ref, ...), custom_call_target="tpu_custom_call", output_to_operand_aliasing={{1}: (7, {}), {2}: (8, {}), {3}: (9, {})} | custom-call | tf_op jit(solution)/shard_map/inverse/pallas_call | solution.py:389
  101.2 19.8 %all_to_all.23 = bf16[32,1,32,256]{3,2,1,0:T(8,128)(2,1)S(1)} all-to-all(bf16[32,1,32,256]{3,2,1,0:T(8,128)(2,1)S(1)} %bitcast.18), channel_id=1, replica_groups=mesh['seq'=16,'batch'=2] {'batch','seq'}, dimensions={0} | all-to-all | bytes 1048576 | tf_op jit(solution)/shard_map/all_to_all | solution.py:509
  120.9 0.9 unpack.1
Async XLA Ops:
  0.6 36.0 %copy-start.4 = (bf16[512,512]{1,0:T(8,128)(2,1)S(1)}, bf16[512,512]{1,0:T(8,128)(2,1)}, u32[]{:S(2)}) copy-start(bf16[512,512]{1,0:T(8,128)(2,1)} %constant.7.clone.matrix_ref) | copy-start | bytes 1572868
  0.6 35.9 %copy-start.5 = (f32[17,2,256]{2,1,0:T(2,128)S(1)}, f32[17,2,256]{2,1,0:T(2,128)}, u32[]{:S(2)}) copy-start(f32[17,2,256]{2,1,0:T(2,128)} %constant.6.clone.twist_ref) | copy-start | bytes 104452
  0.7 66.4 %copy-start.2 = (f32[2,2,256,512]{3,2,1,0:T(8,128)S(1)}, f32[2,2,256,512]{3,2,1,0:T(8,128)}, u32[]{:S(2)}) copy-start(f32[2,2,256,512]{3,2,1,0:T(8,128)} %second_ref.1) | copy-start | bytes 6291460
  2.3 64.8 %copy-start.1 = (f32[2,2,256,512]{3,2,1,0:T(8,128)S(1)}, f32[2,2,256,512]{3,2,1,0:T(8,128)}, u32[]{:S(2)}) copy-start(f32[2,2,256,512]{3,2,1,0:T(8,128)} %first_ref.1) | copy-start | bytes 6291460
  36.6 30.5 %copy-start = (f32[2,2,256,512]{3,2,1,0:T(8,128)S(1)}, f32[2,2,256,512]{3,2,1,0:T(8,128)}, u32[]{:S(2)}) copy-start(f32[2,2,256,512]{3,2,1,0:T(8,128)} %spec_ref.1) | copy-start | bytes 6291460
  69.8 29.7 %copy-start.3 = (bf16[512,512]{1,0:T(8,128)(2,1)S(1)}, bf16[512,512]{1,0:T(8,128)(2,1)}, u32[]{:S(2)}) copy-start(bf16[512,512]{1,0:T(8,128)(2,1)} %constant.8.clone.matrix_ref) | copy-start | bytes 1572868

commit v7 on v6

--- a/solution.py
+++ b/solution.py
@@ -266,47 +266,54 @@
 def moved(grad, spec, first, second):
     new_first = 0.9 * first + 0.1 * grad
     new_second = 0.99 * second + 0.01 * grad * grad
-    return spec - step_rate * jnp.tanh(new_first / (jnp.sqrt(new_second) + epsilon)), new_first, new_second
+    root = new_second * lax.rsqrt(new_second)
+    return spec - step_rate * jnp.tanh(new_first / (root + epsilon)), new_first, new_second
 
 
 def is_mirrored(row, local_outer):
     return lax.axis_index("seq") * local_outer + row > lax.axis_size("seq")
 
 
+early_blocks = 2
+
+
+def state_blocks(parts, local_outer):
+    return [(part, row) for row in range(local_outer) for part in range(parts)]
+
+
 def update_kernel(grad_ref, spec_ref, first_ref, second_ref, *refs):
     final, held, (out_ref, *ready, leaving) = refs[:3], refs[3:6], refs[6:]
-    _, local_outer, points, width = spec_ref.shape
-    early = ready[0].shape[1]
+    parts, local_outer, points, width = spec_ref.shape
     copies = []
-    for row in range(local_outer):
-        eye = square_eye(points, is_mirrored(row, local_outer))
-        for part in range(2):
-            sent = grad_ref[:, row, part].reshape(width, points)
-            grad = lax.dot_general(eye, sent, both_last, preferred_element_type=jnp.float32)
-            made = moved(grad, spec_ref[part, row], first_ref[part, row], second_ref[part, row])
-            for index in range(3):
-                if row < early:
-                    ready[index][part, row] = made[index]
-                    copies.append(
-                        pltpu.make_async_copy(
-                            ready[index].at[part, row], final[index].at[part, row], leaving.at[index, part, row]
-                        )
+    for order, (part, row) in enumerate(state_blocks(parts, local_outer)):
+        if part == 0:
+            eye = square_eye(points, is_mirrored(row, local_outer))
+        sent = grad_ref[:, row, part].reshape(width, points)
+        grad = lax.dot_general(eye, sent, both_last, preferred_element_type=jnp.float32)
+        made = moved(grad, spec_ref[part, row], first_ref[part, row], second_ref[part, row])
+        for index in range(3):
+            if order < early_blocks:
+                ready[index][order] = made[index]
+                copies.append(
+                    pltpu.make_async_copy(
+                        ready[index].at[order], final[index].at[part, row], leaving.at[index, order]
                     )
-                    copies[-1].start()
-                else:
-                    held[index][part, row - early] = made[index]
-            turned = lax.dot_general(
-                made[0].astype(jnp.bfloat16), eye, both_first, preferred_element_type=jnp.float32
-            )
-            out_ref[:, row, part] = turned.astype(jnp.bfloat16).reshape(grad_ref.shape[0], -1, points)
+                )
+                copies[-1].start()
+            else:
+                held[index][order - early_blocks] = made[index]
+        turned = lax.dot_general(
+            made[0].astype(jnp.bfloat16), eye, both_first, preferred_element_type=jnp.float32
+        )
+        out_ref[:, row, part] = turned.astype(jnp.bfloat16).reshape(grad_ref.shape[0], -1, points)
     for copy in copies:
         copy.wait()
 
 
 def update_call(sent, spectrum, first_moment, second_moment):
     parts, local_outer, points, channels = spectrum.shape
-    early = (local_outer + 1) // 2
-    late = (parts, local_outer - early, points, channels)
+    early = (early_blocks, points, channels)
+    late = (parts * local_outer - early_blocks, points, channels)
     made = pl.pallas_call(
         update_kernel,
         in_specs=[whole, whole, whole, whole],
@@ -314,8 +321,7 @@
         out_shape=[jax.ShapeDtypeStruct(spectrum.shape, jnp.float32)] * 3
         + [jax.ShapeDtypeStruct(late, jnp.float32)] * 3
         + [jax.ShapeDtypeStruct(sent.shape, jnp.bfloat16)],
-        scratch_shapes=[pltpu.VMEM((parts, early, points, channels), jnp.float32)] * 3
-        + [pltpu.SemaphoreType.DMA((3, parts, early))],
+        scratch_shapes=[pltpu.VMEM(early, jnp.float32)] * 3 + [pltpu.SemaphoreType.DMA((3, early_blocks))],
         compiler_params=roomy,
         name="update",
     )(sent, spectrum, first_moment, second_moment)
@@ -324,11 +330,11 @@
 
 def inverse_kernel(spectra_ref, filter_ref, twist_ref, matrix_ref, *refs, chunk):
     held, out_ref, final, mid_ref, leaving = refs[:3], refs[6], refs[7:10], refs[10], refs[11]
-    early = final[0].shape[1] - held[0].shape[1]
+    late = state_blocks(*final[0].shape[:2])[early_blocks:]
     pairs = [
-        (source.at[part], target.at[part, early:])
+        (source.at[order], target.at[part, row])
         for source, target in zip(held, final)
-        for part in range(source.shape[0])
+        for order, (part, row) in enumerate(late)
     ]
     copies = copies_of(pairs, leaving, 1)
     for copy in copies:
@@ -395,7 +401,7 @@
         input_output_aliases={7: 1, 8: 2, 9: 3},
         scratch_shapes=[
             pltpu.VMEM((residues, 2, rows, points), jnp.float32),
-            pltpu.SemaphoreType.DMA((6, 1)),
+            pltpu.SemaphoreType.DMA((3 * held[0].shape[0], 1)),
         ],
         compiler_params=roomy,
         name="inverse",

time: 122 us -> 122 us (level)
  no operation moved by 1% of the time
where the time goes in v7:
time: 122 us
  blocking collectives  111 us (91%)
  Pallas kernels  9.93 us (8%)
    all_to_all x1, blocking collectives, per_device(): lax.all_to_all(packed, ('batch', 'seq'), split_axis=0, concat_axis=0, til...  34.3 us
    all_to_all x1, blocking collectives, per_device(): lax.all_to_all(filters, 'seq', split_axis=0, concat_axis=0, tiled=True)  29.6 us
    all_to_all x1, blocking collectives, per_device(): sent = lax.all_to_all(grad, 'seq', split_axis=0, concat_axis=0, tiled=True)  27.4 us
    all_to_all x1, blocking collectives, per_device(): lax.all_to_all(rows, ('batch', 'seq'), split_axis=0, concat_axis=0, tiled...  19.8 us
    pallas_call x1, Pallas kernels, forward_call(): pl.pallas_call(functools.partial(forward_kernel, scale=1.0 / (outer * poi...  3.03 us
    pallas_call x1, Pallas kernels, update_call(): pl.pallas_call(update_kernel, in_specs=[whole, whole, whole, whole], out_...  2.67 us

profile of v7, /device:TPU:0, one launch (start us, length us, event | category | flops | bytes accessed | tf_op | source)
XLA Modules:
  0.0 121.8 jit_solution(6430115181370285698)
XLA Ops:
  0.6 0.0 copy-start.4
  0.6 0.0 copy-start.5
  0.7 0.0 copy-start.2
  0.7 1.6 %pack.1 = bf16[32,64,256]{2,1,0:T(8,128)(2,1)S(1)} custom-call(bf16[256,1024]{1,0:T(8,128)(2,1)} %bitcast.20, bf16[256,1024]{1,0:T(8,128)(2,1)} %bitcast.21), custom_call_target="tpu_custom_call" | custom-call | tf_op jit(solution)/shard_map/pack/pallas_call | solution.py:141
  2.3 0.0 copy-start.1
  2.3 34.3 %all_to_all.20 = bf16[32,1,64,256]{3,2,1,0:T(8,128)(2,1)S(1)} all-to-all(bf16[32,1,64,256]{3,2,1,0:T(8,128)(2,1)S(1)} %bitcast.14), channel_id=1, replica_groups=mesh['seq'=16,'batch'=2] {'batch','seq'}, dimensions={0} | all-to-all | bytes 2097152 | tf_op jit(solution)/shard_map/all_to_all | solution.py:498
  36.6 0.0 copy-start
  36.6 0.0 copy-done.4
  36.6 0.0 copy-done.5
  36.6 3.0 %forward.1 = (bf16[32,2,32,256]{3,2,1,0:T(8,128)(2,1)S(1)}, f32[17,2,64,256]{3,2,1,0:T(8,128)S(1)}) custom-call(bf16[2,16,64,256]{3,2,1,0:T(8,128)(2,1)S(1)} %bitcast.13, f32[17,2,256]{2,1,0:T(2,128)S(1)} %copy-done.5, bf16[512,512]{1,0:T(8,128)(2,1)S(1)} %copy-done.4), custom_call_target="tpu_custom_call" | custom-call | tf_op jit(solution)/shard_map/forward/pallas_call | solution.py:252
  39.6 27.4 %all_to_all.21.grad_ref = bf16[16,2,2,32,256]{4,3,2,1,0:T(8,128)(2,1)S(1)} all-to-all(bf16[16,2,2,32,256]{4,3,2,1,0:T(8,128)(2,1)S(1)} %bitcast.17), channel_id=1, replica_groups=mesh['seq'=16,'batch'=2] {'seq'}, dimensions={0} | all-to-all | bytes 2097152 | tf_op jit(solution)/shard_map/all_to_all | solution.py:505
  67.0 0.0 copy-done.2
  67.0 0.0 copy-done.1
  67.0 0.0 copy-done
  67.0 2.7 %update.1 = (f32[2,2,256,512]{3,2,1,0:T(8,128)}, f32[2,2,256,512]{3,2,1,0:T(8,128)}, f32[2,2,256,512]{3,2,1,0:T(8,128)}, f32[2,256,512]{2,1,0:T(8,128)S(1)}, f32...) custom-call(bf16[16,2,2,32,256]{4,3,2,1,0:T(8,128)(2,1)S(1)} %all_to_all.21.grad_ref, ...), custom_call_target="tpu_custom_call" | custom-call | tf_op jit(solution)/shard_map/update/pallas_call | solution.py:317
  69.7 0.0 copy-start.3
  69.7 29.6 %all_to_all.22 = bf16[16,2,2,32,256]{4,3,2,1,0:T(8,128)(2,1)S(1)} all-to-all(bf16[16,2,2,32,256]{4,3,2,1,0:T(8,128)(2,1)S(1)} %get-tuple-element.19), channel_id=1, replica_groups=mesh['seq'=16,'batch'=2] {'seq'}, dimensions={0} | all-to-all | bytes 2097152 | tf_op jit(solution)/shard_map/all_to_all | solution.py:509
  99.4 0.0 copy-done.3
  99.4 1.7 %inverse.1 = (bf16[2,16,32,256]{3,2,1,0:T(8,128)(2,1)S(1)}, f32[2,2,256,512]{3,2,1,0:T(8,128)}, f32[2,2,256,512]{3,2,1,0:T(8,128)}, f32[2,2,256,512]{3,2,1,0:T(8,128)}) custom-call(f32[17,2,64,256]{3,2,1,0:T(8,128)S(1)} %get-tuple-element.17.spectra_ref, ...), custom_call_target="tpu_custom_call", output_to_operand_aliasing={{1}: (7, {}), {2}: (8, {}), {3}: (9, {})} | custom-call | tf_op jit(solution)/shard_map/inverse/pallas_call | solution.py:395
  101.1 19.8 %all_to_all.23 = bf16[32,1,32,256]{3,2,1,0:T(8,128)(2,1)S(1)} all-to-all(bf16[32,1,32,256]{3,2,1,0:T(8,128)(2,1)S(1)} %bitcast.18), channel_id=1, replica_groups=mesh['seq'=16,'batch'=2] {'batch','seq'}, dimensions={0} | all-to-all | bytes 1048576 | tf_op jit(solution)/shard_map/all_to_all | solution.py:515
  120.9 0.9 unpack.1
Async XLA Ops:
  0.6 36.0 %copy-start.4 = (bf16[512,512]{1,0:T(8,128)(2,1)S(1)}, bf16[512,512]{1,0:T(8,128)(2,1)}, u32[]{:S(2)}) copy-start(bf16[512,512]{1,0:T(8,128)(2,1)} %constant.7.clone.matrix_ref) | copy-start | bytes 1572868
  0.6 35.9 %copy-start.5 = (f32[17,2,256]{2,1,0:T(2,128)S(1)}, f32[17,2,256]{2,1,0:T(2,128)}, u32[]{:S(2)}) copy-start(f32[17,2,256]{2,1,0:T(2,128)} %constant.6.clone.twist_ref) | copy-start | bytes 104452
  0.7 66.4 %copy-start.2 = (f32[2,2,256,512]{3,2,1,0:T(8,128)S(1)}, f32[2,2,256,512]{3,2,1,0:T(8,128)}, u32[]{:S(2)}) copy-start(f32[2,2,256,512]{3,2,1,0:T(8,128)} %second_ref.1) | copy-start | bytes 6291460
  2.3 64.8 %copy-start.1 = (f32[2,2,256,512]{3,2,1,0:T(8,128)S(1)}, f32[2,2,256,512]{3,2,1,0:T(8,128)}, u32[]{:S(2)}) copy-start(f32[2,2,256,512]{3,2,1,0:T(8,128)} %first_ref.1) | copy-start | bytes 6291460
  36.6 30.5 %copy-start = (f32[2,2,256,512]{3,2,1,0:T(8,128)S(1)}, f32[2,2,256,512]{3,2,1,0:T(8,128)}, u32[]{:S(2)}) copy-start(f32[2,2,256,512]{3,2,1,0:T(8,128)} %spec_ref.1) | copy-start | bytes 6291460
  69.7 29.7 %copy-start.3 = (bf16[512,512]{1,0:T(8,128)(2,1)S(1)}, bf16[512,512]{1,0:T(8,128)(2,1)}, u32[]{:S(2)}) copy-start(bf16[512,512]{1,0:T(8,128)(2,1)} %constant.8.clone.matrix_ref) | copy-start | bytes 1572868
